TPU v7x, 256 devices: a whole 4x4x8 slice. The times are simulated.
256 devices in a mesh: gx: 32 (over z, y), gy: 8 (over x, core).
Axes of the slice: x: 4, y: 4, z: 8, core: 2. Of those that a mesh axis runs over, the one named last changes fastest.
Arguments:
- e_adj: float32 [3, 8, 2048, 2048], P(None, None, 'gx', 'gy'), may hold values from -6 to 6
- h_adj: float32 [3, 8, 2048, 2048], P(None, None, 'gx', 'gy'), may hold values from -6 to 6
- density: float32 [2048, 2048], P('gx', 'gy'), may hold values from 0.05 to 0.95
- material: int32 [8, 2048, 2048], P(None, 'gx', 'gy'), may hold values from 0 to 3
- eps_table: float32 [4], replicated, may hold values from 1 to 12
- dft_adj: float32 [4, 2, 3, 2, 2048, 2048], P(None, None, None, None, 'gx', 'gy'), may hold values from -6 to 6
- dft_fwd: bfloat16 [4, 2, 3, 2, 2048, 2048], P(None, None, None, None, 'gx', 'gy'), may hold values from -6 to 6
- tile_map: int32 [32, 32], P('gx', 'gy'), may hold values from 0 to 255, as said below
Outputs:
- e_out: float32 [3, 8, 2048, 2048], P(None, None, 'gx', 'gy')
- h_out: float32 [3, 8, 2048, 2048], P(None, None, 'gx', 'gy')
- param_grad: float32 [256, 4096], P(('gx', 'gy'))
Inputs may be any that keep to these rules, and one draw needn't show every extreme that they name: `tile_map`: each of the 256 design parameters is named by exactly 4 tiles. Parameter p belongs to the device at position p // (256 / number of devices) in the gx-major order of devices.
All inputs are finite; a program needn't handle non-finite values.
Results may differ from a plain program's by a relative error of at most 0.0003.
Values sent between devices are 32-bit elements; how exact they have to be, the bound alone decides.
A program may use at most 64 MiB of HBM per device.

v0:
```python
import jax
import jax.numpy as jnp
from jax import lax
from jax.sharding import PartitionSpec as P

PLANES = 2
ZLO = 3
STEPS = 2
FREQ = 4
PML = 12
MATS = 4
TILE = 64
REPEAT = 4


courant = 0.5
sigma_peak = 0.8
dft_weight = 0.5
sharpness = 4.0
threshold = 0.5
eps_low = 2.1
eps_high = 12.1
grad_scale = 0.01


def with_halo(cells, sides, width):
    for axis, dim in sides:
        count = lax.axis_size(axis)
        ends = count - 1
        head = lax.slice_in_dim(cells, 0, width, axis=dim)
        tail = lax.slice_in_dim(cells, cells.shape[dim] - width, cells.shape[dim], axis=dim)
        cells = jnp.concatenate(
            [
                lax.ppermute(tail, axis, [(i, (i + 1) % count) for i in range(ends)]),
                cells,
                lax.ppermute(head, axis, [((i + 1) % count, i) for i in range(ends)]),
            ],
            axis=dim,
        )
    return cells


def shifted(block, axis, distance):
    devices = range(lax.axis_size(axis))
    route = [(i - distance, i) for i in devices if i - distance in devices]
    return lax.ppermute(block, axis, route)


def positions(offset_index, count_cells):
    return (offset_index * count_cells + jnp.arange(count_cells, dtype=jnp.int32)).astype(
        jnp.float32
    )


def profile(places, total):
    depth = jnp.maximum(jnp.maximum(PML - places, places - (total - 1 - PML)), 0.0) / PML
    return depth * depth * depth


def smooth(grid_field):
    padded = with_halo(grid_field, (("gx", 0), ("gy", 1)), 1)
    summed = padded[:-2] + 2.0 * padded[1:-1] + padded[2:]
    return (summed[:, :-2] + 2.0 * summed[:, 1:-1] + summed[:, 2:]) / 16.0


def step_next(values, border, dim_index):
    inner = lax.slice_in_dim(values, 1, values.shape[dim_index], axis=dim_index)
    return jnp.concatenate([inner, border], axis=dim_index) - values


def step_prev(values, border, dim_index):
    inner = lax.slice_in_dim(values, 0, values.shape[dim_index] - 1, axis=dim_index)
    return values - jnp.concatenate([border, inner], axis=dim_index)


def zero_rim(values, dim_index):
    return jnp.zeros_like(lax.slice_in_dim(values, 0, 1, axis=dim_index))


def next_faces(elec_x, elec_y, elec_z):
    ahead_x = shifted(jnp.stack([elec_y[:, :1, :], elec_z[:, :1, :]]), "gx", -1)
    ahead_y = shifted(jnp.stack([elec_x[:, :, :1], elec_z[:, :, :1]]), "gy", -1)
    return (ahead_x, ahead_y)


def prev_faces(mag_x, mag_y, mag_z):
    behind_x = shifted(jnp.stack([mag_y[:, -1:, :], mag_z[:, -1:, :]]), "gx", 1)
    behind_y = shifted(jnp.stack([mag_x[:, :, -1:], mag_z[:, :, -1:]]), "gy", 1)
    return (behind_x, behind_y)


def curl_forward(elec_x, elec_y, elec_z, ahead_x, ahead_y):
    curl_x = step_next(elec_z, ahead_y[1], 2) - step_next(elec_y, zero_rim(elec_y, 0), 0)
    curl_y = step_next(elec_x, zero_rim(elec_x, 0), 0) - step_next(elec_z, ahead_x[1], 1)
    curl_z = step_next(elec_y, ahead_x[0], 1) - step_next(elec_x, ahead_y[0], 2)
    return (curl_x, curl_y, curl_z)


def curl_backward(mag_x, mag_y, mag_z, behind_x, behind_y):
    curl_x = step_prev(mag_z, behind_y[1], 2) - step_prev(mag_y, zero_rim(mag_y, 0), 0)
    curl_y = step_prev(mag_x, zero_rim(mag_x, 0), 0) - step_prev(mag_z, behind_x[1], 1)
    curl_z = step_prev(mag_y, behind_x[0], 1) - step_prev(mag_x, behind_y[0], 2)
    return (curl_x, curl_y, curl_z)


def accumulate(accum, elec_x, elec_y, elec_z, step_index):
    design = jnp.stack([elec_x, elec_y, elec_z])[:, ZLO : ZLO + PLANES]
    angular = 0.21 + 0.06 * jnp.arange(FREQ, dtype=jnp.float32)
    turned = angular * (step_index + 1)
    weights = jnp.stack([dft_weight * jnp.cos(turned), -dft_weight * jnp.sin(turned)], axis=1)
    return accum + weights[:, :, None, None, None, None] * design[None, None]


def on_device(e_adj, h_adj, density, material, eps_table, dft_adj, dft_fwd, tile_map):
    planes_z, width_x, width_y = material.shape
    count_gx = lax.axis_size("gx")
    count_gy = lax.axis_size("gy")
    total_x = count_gx * width_x
    total_y = count_gy * width_y
    sigma = sigma_peak * (
        profile(positions(lax.axis_index("gx"), width_x), total_x)[:, None]
        + profile(positions(lax.axis_index("gy"), width_y), total_y)[None, :]
    )
    half_sum = 1.0 + 0.5 * sigma
    damping = (1.0 - 0.5 * sigma) / half_sum
    coef_h = courant / half_sum
    filtered = smooth(density)
    bend_value = jnp.tanh(sharpness * (filtered - threshold))
    scale_sum = jnp.tanh(sharpness * threshold) + jnp.tanh(sharpness * (1.0 - threshold))
    projected = (jnp.tanh(sharpness * threshold) + bend_value) / scale_sum
    slope = sharpness * (1.0 - bend_value * bend_value) / scale_sum
    design_eps = eps_low + (eps_high - eps_low) * projected
    eps_grid = jnp.zeros(material.shape, jnp.float32)
    for material_id in range(MATS):
        eps_grid = jnp.where(material == material_id, eps_table[material_id], eps_grid)
    layer_ids = jnp.arange(planes_z, dtype=jnp.int32)[:, None, None]
    inside = (layer_ids >= ZLO) & (layer_ids < ZLO + PLANES)
    eps_grid = jnp.where(inside, design_eps[None], eps_grid)
    coef_e = courant / (eps_grid * half_sum[None])
    elec_x, elec_y, elec_z = (e_adj[0], e_adj[1], e_adj[2])
    mag_x, mag_y, mag_z = (h_adj[0], h_adj[1], h_adj[2])
    accum = dft_adj
    for step_index in range(STEPS):
        ahead_x, ahead_y = next_faces(elec_x, elec_y, elec_z)
        curl_x, curl_y, curl_z = curl_forward(elec_x, elec_y, elec_z, ahead_x, ahead_y)
        mag_x = damping * mag_x - coef_h * curl_x
        mag_y = damping * mag_y - coef_h * curl_y
        mag_z = damping * mag_z - coef_h * curl_z
        behind_x, behind_y = prev_faces(mag_x, mag_y, mag_z)
        curl_x, curl_y, curl_z = curl_backward(mag_x, mag_y, mag_z, behind_x, behind_y)
        elec_x = damping * elec_x + coef_e * curl_x
        elec_y = damping * elec_y + coef_e * curl_y
        elec_z = damping * elec_z + coef_e * curl_z
        accum = accumulate(accum, elec_x, elec_y, elec_z, step_index)
    forward = dft_fwd.astype(jnp.float32)
    intersection = jnp.sum(
        forward[:, 0] * accum[:, 0] - forward[:, 1] * accum[:, 1], axis=(0, 1, 2)
    )
    local_grad = grad_scale * (eps_high - eps_low) * slope * intersection
    grad_cells = smooth(local_grad)
    tile_rows = (
        grad_cells.reshape(width_x // TILE, TILE, width_y // TILE, TILE)
        .transpose(0, 2, 1, 3)
        .reshape(-1, TILE * TILE)
    )
    owners = tile_map.reshape(-1)
    devices_all = count_gx * count_gy
    params_all = total_x // TILE * (total_y // TILE) // REPEAT
    rows_mine = params_all // devices_all
    labels = jnp.arange(rows_mine * lax.axis_size(("gx", "gy")), dtype=jnp.int32)
    one_hot = (labels[:, None] == owners[None, :]).astype(jnp.float32)
    param_grad = lax.psum_scatter(
        jnp.dot(
            one_hot, tile_rows, precision=lax.Precision.HIGHEST, preferred_element_type=jnp.float32
        ),
        ("gx", "gy"),
        scatter_dimension=0,
        tiled=True,
    )
    return (jnp.stack([elec_x, elec_y, elec_z]), jnp.stack([mag_x, mag_y, mag_z]), param_grad)


def solution(mesh):
    in_specs = (
        P(None, None, "gx", "gy"),
        P(None, None, "gx", "gy"),
        P("gx", "gy"),
        P(None, "gx", "gy"),
        P(),
        P(None, None, None, None, "gx", "gy"),
        P(None, None, None, None, "gx", "gy"),
        P("gx", "gy"),
    )
    out_specs = (P(None, None, "gx", "gy"), P(None, None, "gx", "gy"), P(("gx", "gy"), None))
    return jax.shard_map(
        on_device, mesh=mesh, in_specs=in_specs, out_specs=out_specs, check_vma=False
    )
```

profile of v0, /device:TPU:1, one launch (start us, length us, event | category | flops | bytes accessed | tf_op | source)
XLA Modules:
  0.0 433.0 jit_solution(10354601674597787234)
XLA Ops:
  7.2 1.5 fusion.60
  9.4 1.3 collective-permute-start.4
  12.0 5.1 %collective-permute-start.5 = (f32[2,8,64,1]{2,1,3,0:T(8,128)}, f32[2,8,64,1]{2,1,3,0:T(8,128)}, u32[]{:S(2)}, u32[]{:S(2)}) collective-permute-start(f32[2,8,64,1]{2,1,3,0:T(8,128)} %pad_maximum_fusion.12), channel_id=1, source_target_pairs={{1,0},{2,1},{3,2},{4,3},{5,4},{6,5},{7,6},{9,8},{10,9},{11,10},{12... | collective-permute-start | bytes 12296 | tf_op jit(solution)/shard_map/ppermute | solution.py:46
  17.8 4.3 collective-permute-start
  22.1 1.3 collective-permute-start.1
  23.4 2.2 fusion.58
  25.7 2.6 fusion.59
  29.1 1.5 copy_bitcast_fusion
  32.0 1.0 slice.394
  33.0 0.8 slice.400
  33.9 1.9 collective-permute-start.2
  35.9 2.4 collective-permute-start.3
  38.3 1.0 slice.390
  39.3 0.9 slice.386
  40.1 2.0 convert_element_type.20
  43.1 0.9 copy.262
  44.0 0.9 copy.264
  44.9 4.5 %fusion.7 = (f32[8,64,256]{2,0,1:T(8,128)S(1)}, f32[8,64,256]{2,0,1:T(8,128)S(1)}, f32[8,64,256]{2,0,1:T(8,128)S(1)}) fusion(f32[8,64,1]{2,0,1:T(8,128)} %copy.264, f32[8,64,255]{2,0,1:T(8,128)} %slice.394, f32[1,8,64,256]{3,2,1,0:T(8,128)} %get-tuple-element.26, f32[7,64,256]{2,0,1:T(8,128)} %get-tuple-element.70, f32[64,256]{1,0:T(8,128)S(1)} %get-tuple-element.63, ...), kind=kLoop, calls=%fused_computation.15 | loop fusion | flops 2883584 | bytes 7864320 | tf_op jit(solution)/shard_map/sub | solution.py:146
  50.0 3.2 collective-permute-start.6
  54.9 4.0 collective-permute-start.7
  58.9 0.9 copy.268
  59.7 4.4 %fusion.10 = f32[8,64,256]{2,0,1:T(8,128)S(1)} fusion(f32[8,64,256]{2,0,1:T(8,128)S(1)} %get-tuple-element.37, f32[8,64,255]{2,0,1:T(8,128)S(1)} %bitcast.138, f32[8,64,1]{2,0,1:T(8,128)} %copy.268, f32[8,64,256]{2,0,1:T(8,128)S(1)} %get-tuple-element.36, f32[7,64,256]{2,0,1:T(8,128)S(1)} %bitcast.147, f32[64,256]{1,0:T(8,128)S(1)} %get-tuple-element.64, ...), kind=kLoop, calls=%fused_computation.19 | loop fusion | flops 2359296 | bytes 3801112 | tf_op jit(solution)/shard_map/add | solution.py:151
  64.1 1.0 slice.416
  65.1 0.9 slice.427
  66.0 0.9 copy.271
  67.1 4.8 %fusion.19 = f32[8,64,256]{2,0,1:T(8,128)S(1)} fusion(f32[8,64,256]{2,0,1:T(8,128)S(1)} %get-tuple-element.36, f32[8,63,256]{2,0,1:T(8,128)} %slice.411, f32[8,1,256]{2,0,1:T(8,128)S(1)} %get-tuple-element.51, f32[8,64,256]{2,0,1:T(8,128)S(1)} %get-tuple-element.35, f32[8,64,255]{2,0,1:T(8,128)S(1)} %bitcast.136, f32[8,64,1]{2,0,1:T(8,128)} %copy.271, ...), kind=kLoop, calls=%fused_computation.31 | loop fusion | flops 2490368 | bytes 3866648 | tf_op jit(solution)/shard_map/add | solution.py:153
  72.6 3.5 fusion.16
  76.1 1.3 copy.273
  77.3 1.9 collective-permute-start.9
  79.5 0.9 slice.422
  80.3 0.9 slice.408
  81.2 1.0 slice.420
  83.8 1.3 collective-permute-start.8
  85.1 0.9 copy.274
  86.0 0.9 copy.275
  86.9 1.4 collective-permute-done.8
  88.3 3.6 fusion.25
  91.9 0.8 slice.424
  92.7 0.8 slice.423
  93.6 1.1 copy.276
  94.7 1.1 copy.277
  95.8 5.0 %collective-permute-start.10 = (f32[2,8,64,1]{2,1,3,0:T(8,128)S(1)}, f32[2,8,64,1]{2,1,3,0:T(8,128)S(1)}, u32[]{:S(2)}, u32[]{:S(2)}) collective-permute-start(f32[2,8,64,1]{2,1,3,0:T(8,128)S(1)} %pad_maximum_fusion.15), channel_id=1, source_target_pairs={{0,1},{1,2},{2,3},{3,4},{4,5},{5,6},{6,7},{8,9},{9,10},{10,11},{11... | collective-permute-start | bytes 12296 | tf_op jit(solution)/shard_map/ppermute | solution.py:46
  100.8 0.8 slice.435
  101.7 0.9 slice.437
  102.5 4.1 collective-permute-start.11
  106.6 0.9 copy.278
  107.5 5.3 %fusion.29 = f32[1,8,64,256]{3,1,2,0:T(8,128)} fusion(f32[8,64,256]{2,0,1:T(8,128)S(1)} %get-tuple-element.33, f32[8,64,255]{2,0,1:T(8,128)S(1)} %bitcast.142, f32[8,64,1]{2,0,1:T(8,128)} %copy.278, f32[8,64,256]{2,0,1:T(8,128)} %get-tuple-element.34, f32[7,64,256]{2,0,1:T(8,128)} %bitcast.148, f32[8,64,256]{2,0,1:T(8,128)S(1)} %fusion.10, ...), kind=kLoop, calls=%fused_computation.46 | loop fusion | flops 2359296 | bytes 3801112 | tf_op jit(solution)/shard_map/stack | solution.py:180
  112.8 0.9 copy.279
  113.7 4.3 fusion.36
  118.0 3.2 fusion.40
  121.6 0.9 copy-done.11
  122.6 1.1 copy-done.13
  124.5 1.2 copy-done.7
  126.4 5.8 %collective-permute-start.12 = (f32[1,256]{1,0:T(1,128)S(1)}, f32[1,256]{1,0:T(1,128)S(1)}, u32[]{:S(2)}, u32[]{:S(2)}) collective-permute-start(f32[1,256]{1,0:T(1,128)S(1)} %get-tuple-element.42), channel_id=1, source_target_pairs={{0,8},{8,16},{16,24},{24,32},{32,40},{40,48},{48,56},{56,64},{64,7... | collective-permute-start | bytes 3080 | tf_op jit(solution)/shard_map/ppermute | solution.py:34
  132.2 1.3 collective-permute-start.13
  133.5 5.4 %collective-permute-done.13 = f32[1,256]{1,0:T(1,128)S(1)} collective-permute-done((f32[1,256]{1,0:T(1,128)S(1)}, f32[1,256]{1,0:T(1,128)S(1)}, u32[]{:S(2)}, u32[]{:S(2)}) %collective-permute-start.13) | collective-permute-done | bytes 1056 | tf_op jit(solution)/shard_map/ppermute | solution.py:36
  139.0 3.3 collective-permute-start.14
  142.3 1.9 collective-permute-start.15
  144.3 3.3 collective-permute-done.15
  148.1 3.8 fusion.44
  152.0 1.6 copy.284
  153.7 1.6 copy.283
  155.3 269.3 %all-reduce.11.cloned.1.call-done = f32[256,4096]{1,0:T(8,128)} async-done(((f32[256,4096]{1,0:T(8,128)}), f32[256,4096]{1,0:T(8,128)}) %all-reduce.11.cloned.1.call-update) | async-done | bytes 4194320
  424.6 1.5 constant_dynamic-slice_fusion
  (139 shorter events, 13.4 us)
Async XLA Ops:
  7.2 417.4 %all-reduce.11.cloned.1.call-start = ((), (), s32[]{:S(2)}) async-start(), calls=%async_computation | async-start | bytes 8388608
  8.7 36.2 %copy-start.8 = (f32[1,8,64,256]{3,2,1,0:T(8,128)}, f32[1,8,64,256]{3,2,1,0:T(8,128)S(1)}, u32[]{:S(2)}) copy-start(f32[1,8,64,256]{3,2,1,0:T(8,128)S(1)} %get-tuple-element.31) | copy-start | bytes 1572868
  8.7 36.2 %copy-start.10 = (f32[1,8,64,256]{3,2,1,0:T(8,128)}, f32[1,8,64,256]{3,2,1,0:T(8,128)S(1)}, u32[]{:S(2)}) copy-start(f32[1,8,64,256]{3,2,1,0:T(8,128)S(1)} %get-tuple-element.30) | copy-start | bytes 1572868
  9.4 35.5 %collective-permute-start.4 = (f32[2,8,1,256]{3,1,2,0:T(8,128)S(1)}, f32[2,8,1,256]{3,1,2,0:T(8,128)S(1)}, u32[]{:S(2)}, u32[]{:S(2)}) collective-permute-start(f32[2,8,1,256]{3,1,2,0:T(8,128)S(1)} %pad_maximum_fusion.8), channel_id=1, source_target_pairs={{8,0},{16,8},{24,16},{32,24},{40,32},{48,40},{56,48},{64,56},{72,6... | collective-permute-start | bytes 49160 | tf_op jit(solution)/shard_map/ppermute | solution.py:46
  12.0 30.5 %collective-permute-start.5 = (f32[2,8,64,1]{2,1,3,0:T(8,128)}, f32[2,8,64,1]{2,1,3,0:T(8,128)}, u32[]{:S(2)}, u32[]{:S(2)}) collective-permute-start(f32[2,8,64,1]{2,1,3,0:T(8,128)} %pad_maximum_fusion.12), channel_id=1, source_target_pairs={{1,0},{2,1},{3,2},{4,3},{5,4},{6,5},{7,6},{9,8},{10,9},{11,10},{12... | collective-permute-start | bytes 12296 | tf_op jit(solution)/shard_map/ppermute | solution.py:46
  17.8 16.0 %collective-permute-start = (f32[1,256]{1,0:T(1,128)S(1)}, f32[1,256]{1,0:T(1,128)S(1)}, u32[]{:S(2)}, u32[]{:S(2)}) collective-permute-start(f32[1,256]{1,0:T(1,128)S(1)} %get-tuple-element.44), channel_id=1, source_target_pairs={{0,8},{8,16},{16,24},{24,32},{32,40},{40,48},{48,56},{56,64},{64,7... | collective-permute-start | bytes 3080 | tf_op jit(solution)/shard_map/ppermute | solution.py:34
  22.1 11.8 %collective-permute-start.1 = (f32[1,256]{1,0:T(1,128)S(1)}, f32[1,256]{1,0:T(1,128)S(1)}, u32[]{:S(2)}, u32[]{:S(2)}) collective-permute-start(f32[1,256]{1,0:T(1,128)S(1)} %get-tuple-element.45), channel_id=1, source_target_pairs={{8,0},{16,8},{24,16},{32,24},{40,32},{48,40},{56,48},{64,56},{72,6... | collective-permute-start | bytes 3080 | tf_op jit(solution)/shard_map/ppermute | solution.py:36
  25.7 2.7 copy-start.25
  25.7 3.4 copy-start.17
  25.7 3.4 copy-start.18
  29.1 4.7 %copy-start.22 = (f32[64,256]{1,0:T(8,128)S(1)}, f32[64,256]{1,0:T(8,128)}, u32[]{:S(2)}) copy-start(f32[64,256]{1,0:T(8,128)} %param.10) | copy-start | bytes 196612
  33.0 7.2 %copy-start.20 = (bf16[4,2,3,2,64,256]{5,4,3,2,1,0:T(8,128)(2,1)S(1)}, bf16[4,2,3,2,64,256]{5,4,3,2,1,0:T(8,128)(2,1)}, u32[]{:S(2)}) copy-start(bf16[4,2,3,2,64,256]{5,4,3,2,1,0:T(8,128)(2,1)} %param.14) | copy-start | bytes 4718596
  33.9 8.2 %collective-permute-start.2 = (f32[66,1]{1,0:T(8,128)S(1)}, f32[66,1]{1,0:T(8,128)S(1)}, u32[]{:S(2)}, u32[]{:S(2)}) collective-permute-start(f32[66,1]{1,0:T(8,128)S(1)} %get-tuple-element.40), channel_id=1, source_target_pairs={{0,1},{1,2},{2,3},{3,4},{4,5},{5,6},{6,7},{8,9},{9,10},{10,11},{11... | collective-permute-start | bytes 800 | tf_op jit(solution)/shard_map/ppermute | solution.py:34
  35.9 6.3 %collective-permute-start.3 = (f32[66,1]{1,0:T(8,128)S(1)}, f32[66,1]{1,0:T(8,128)S(1)}, u32[]{:S(2)}, u32[]{:S(2)}) collective-permute-start(f32[66,1]{1,0:T(8,128)S(1)} %get-tuple-element.41), channel_id=1, source_target_pairs={{1,0},{2,1},{3,2},{4,3},{5,4},{6,5},{7,6},{9,8},{10,9},{11,10},{12... | collective-permute-start | bytes 800 | tf_op jit(solution)/shard_map/ppermute | solution.py:36
  49.4 17.6 %copy-start.2 = (f32[8,64,256]{2,0,1:T(8,128)}, f32[8,64,256]{2,0,1:T(8,128)S(1)}, u32[]{:S(2)}) copy-start(f32[8,64,256]{2,0,1:T(8,128)S(1)} %get-tuple-element.36) | copy-start | bytes 1572868
  49.7 10.0 %copy-start.3 = (s32[8,64,256]{2,1,0:T(8,128)S(1)}, s32[8,64,256]{2,1,0:T(8,128)}, u32[]{:S(2)}) copy-start(s32[8,64,256]{2,1,0:T(8,128)} %param.11) | copy-start | bytes 1572868
  50.0 8.8 %collective-permute-start.6 = (f32[2,8,64,1]{2,1,3,0:T(8,128)S(1)}, f32[2,8,64,1]{2,1,3,0:T(8,128)S(1)}, u32[]{:S(2)}, u32[]{:S(2)}) collective-permute-start(f32[2,8,64,1]{2,1,3,0:T(8,128)S(1)} %pad_maximum_fusion.13), channel_id=1, source_target_pairs={{0,1},{1,2},{2,3},{3,4},{4,5},{5,6},{6,7},{8,9},{9,10},{10,11},{11... | collective-permute-start | bytes 12296 | tf_op jit(solution)/shard_map/ppermute | solution.py:46
  54.9 12.2 %collective-permute-start.7 = (f32[2,8,1,256]{3,1,2,0:T(8,128)S(1)}, f32[2,8,1,256]{3,1,2,0:T(8,128)S(1)}, u32[]{:S(2)}, u32[]{:S(2)}) collective-permute-start(f32[2,8,1,256]{3,1,2,0:T(8,128)S(1)} %pad_maximum_fusion.9), channel_id=1, source_target_pairs={{0,8},{8,16},{16,24},{24,32},{32,40},{40,48},{48,56},{56,64},{64,7... | collective-permute-start | bytes 49160 | tf_op jit(solution)/shard_map/ppermute | solution.py:46
  67.0 5.5 %copy-start.9 = (f32[1,8,64,256]{3,2,1,0:T(8,128)S(1)}, f32[1,8,64,256]{3,2,1,0:T(8,128)}, u32[]{:S(2)}) copy-start(f32[1,8,64,256]{3,2,1,0:T(8,128)} %copy-done.8) | copy-start | bytes 1572868
  67.1 5.5 %copy-start.15 = (f32[8,63,256]{2,0,1:T(8,128)S(1)}, f32[8,63,256]{2,0,1:T(8,128)}, u32[]{:S(2)}) copy-start(f32[8,63,256]{2,0,1:T(8,128)} %slice.407) | copy-start | bytes 1548292
  76.0 4.3 copy-start
  77.3 7.7 %collective-permute-start.9 = (f32[2,8,64,1]{2,1,3,0:T(8,128)S(1)}, f32[2,8,64,1]{2,1,3,0:T(8,128)S(1)}, u32[]{:S(2)}, u32[]{:S(2)}) collective-permute-start(f32[2,8,64,1]{2,1,3,0:T(8,128)S(1)} %pad_maximum_fusion.14), channel_id=1, source_target_pairs={{1,0},{2,1},{3,2},{4,3},{5,4},{6,5},{7,6},{9,8},{10,9},{11,10},{12... | collective-permute-start | bytes 12296 | tf_op jit(solution)/shard_map/ppermute | solution.py:46
  83.8 4.5 %collective-permute-start.8 = (f32[2,8,1,256]{3,1,2,0:T(8,128)S(1)}, f32[2,8,1,256]{3,1,2,0:T(8,128)S(1)}, u32[]{:S(2)}, u32[]{:S(2)}) collective-permute-start(f32[2,8,1,256]{3,1,2,0:T(8,128)S(1)} %pad_maximum_fusion.10), channel_id=1, source_target_pairs={{8,0},{16,8},{24,16},{32,24},{40,32},{48,40},{56,48},{64,56},{72,6... | collective-permute-start | bytes 49160 | tf_op jit(solution)/shard_map/ppermute | solution.py:46
  91.9 8.9 %copy-start.5 = (f32[8,64,256]{2,0,1:T(8,128)S(1)}, f32[8,64,256]{2,0,1:T(8,128)}, u32[]{:S(2)}) copy-start(f32[8,64,256]{2,0,1:T(8,128)} %get-tuple-element.34) | copy-start | bytes 1572868
  93.6 13.9 %copy-start.4 = (s32[8,64,256]{2,1,0:T(8,128)S(1)}, s32[8,64,256]{2,1,0:T(8,128)}, u32[]{:S(2)}) copy-start(s32[8,64,256]{2,1,0:T(8,128)} %param.11) | copy-start | bytes 1572868
  95.8 10.8 %collective-permute-start.10 = (f32[2,8,64,1]{2,1,3,0:T(8,128)S(1)}, f32[2,8,64,1]{2,1,3,0:T(8,128)S(1)}, u32[]{:S(2)}, u32[]{:S(2)}) collective-permute-start(f32[2,8,64,1]{2,1,3,0:T(8,128)S(1)} %pad_maximum_fusion.15), channel_id=1, source_target_pairs={{0,1},{1,2},{2,3},{3,4},{4,5},{5,6},{6,7},{8,9},{9,10},{10,11},{11... | collective-permute-start | bytes 12296 | tf_op jit(solution)/shard_map/ppermute | solution.py:46
  102.5 11.2 %collective-permute-start.11 = (f32[2,8,1,256]{3,1,2,0:T(8,128)S(1)}, f32[2,8,1,256]{3,1,2,0:T(8,128)S(1)}, u32[]{:S(2)}, u32[]{:S(2)}) collective-permute-start(f32[2,8,1,256]{3,1,2,0:T(8,128)S(1)} %pad_maximum_fusion.11), channel_id=1, source_target_pairs={{0,8},{8,16},{16,24},{24,32},{32,40},{40,48},{48,56},{56,64},{64,7... | collective-permute-start | bytes 49160 | tf_op jit(solution)/shard_map/ppermute | solution.py:46
  107.5 6.2 %copy-start.1 = (f32[8,64,256]{2,0,1:T(8,128)S(1)}, f32[8,64,256]{2,0,1:T(8,128)}, u32[]{:S(2)}) copy-start(f32[8,64,256]{2,0,1:T(8,128)} %copy-done) | copy-start | bytes 1572868
  113.7 4.3 copy-start.6
  113.7 4.3 copy-start.16
  113.7 4.3 copy-start.21
  118.0 3.3 copy-start.14
  121.3 2.5 copy-start.13
  121.4 1.1 copy-start.11
  121.4 2.4 copy-start.19
  121.4 2.3 copy-start.23
  121.5 2.3 copy-start.24
  123.8 1.9 copy-start.7
  126.3 21.8 %copy-start.26 = (s32[1,4]{1,0:T(1,128)S(1)}, s32[1,4]{1,0:T(1,128)}, u32[]{:S(2)}) copy-start(s32[1,4]{1,0:T(1,128)} %param.15) | copy-start | bytes 52
  126.4 7.1 %collective-permute-start.12 = (f32[1,256]{1,0:T(1,128)S(1)}, f32[1,256]{1,0:T(1,128)S(1)}, u32[]{:S(2)}, u32[]{:S(2)}) collective-permute-start(f32[1,256]{1,0:T(1,128)S(1)} %get-tuple-element.42), channel_id=1, source_target_pairs={{0,8},{8,16},{16,24},{24,32},{32,40},{40,48},{48,56},{56,64},{64,7... | collective-permute-start | bytes 3080 | tf_op jit(solution)/shard_map/ppermute | solution.py:34
  132.2 6.7 %collective-permute-start.13 = (f32[1,256]{1,0:T(1,128)S(1)}, f32[1,256]{1,0:T(1,128)S(1)}, u32[]{:S(2)}, u32[]{:S(2)}) collective-permute-start(f32[1,256]{1,0:T(1,128)S(1)} %get-tuple-element.43), channel_id=1, source_target_pairs={{8,0},{16,8},{24,16},{32,24},{40,32},{48,40},{56,48},{64,56},{72,6... | collective-permute-start | bytes 3080 | tf_op jit(solution)/shard_map/ppermute | solution.py:36
  139.0 5.3 %collective-permute-start.14 = (f32[66,1]{1,0:T(8,128)S(1)}, f32[66,1]{1,0:T(8,128)S(1)}, u32[]{:S(2)}, u32[]{:S(2)}) collective-permute-start(f32[66,1]{1,0:T(8,128)S(1)} %get-tuple-element.38), channel_id=1, source_target_pairs={{0,1},{1,2},{2,3},{3,4},{4,5},{5,6},{6,7},{8,9},{9,10},{10,11},{11... | collective-permute-start | bytes 800 | tf_op jit(solution)/shard_map/ppermute | solution.py:34
  142.3 5.3 %collective-permute-start.15 = (f32[66,1]{1,0:T(8,128)S(1)}, f32[66,1]{1,0:T(8,128)S(1)}, u32[]{:S(2)}, u32[]{:S(2)}) collective-permute-start(f32[66,1]{1,0:T(8,128)S(1)} %get-tuple-element.39), channel_id=1, source_target_pairs={{1,0},{2,1},{3,2},{4,3},{5,4},{6,5},{7,6},{9,8},{10,9},{11,10},{12... | collective-permute-start | bytes 800 | tf_op jit(solution)/shard_map/ppermute | solution.py:36
  152.0 1.6 copy-start.12
Sparse Core Ops, SparseCore 0:
  152.0 272.5 all-reduce.10
where the time goes:
time: 435 us; the launch traced here: 433 us
  waiting for transfers between devices  279 us (64%)
  starting transfers between devices  48 us (11%)
  local copies, waits for them, and re-layouts  46.8 us (11%)
  other arithmetic  40 us (9%)
  between operations  14.9 us (3%)
    unnamed x2, waiting for transfers between devices  269 us
    ppermute x8, starting transfers between devices, shifted(): return lax.ppermute(block, axis, route)  25.8 us
    ppermute x4, starting transfers between devices, with_halo(): lax.ppermute(tail, axis, [(i, (i + 1) % count) for i in range(ends)])  15.3 us
    another operation x4, other arithmetic, on_device(): jnp.stack([elec_x, elec_y, elec_z])  12.9 us
    slice x12, local copies, waits for them, and re-layouts, step_next(): inner = lax.slice_in_dim(values, 1, values.shape[dim_index], axis=dim_index)  12.8 us
    unnamed x60, local copies, waits for them, and re-layouts  9.12 us
    ppermute x4, waiting for transfers between devices, with_halo(): lax.ppermute(head, axis, [((i + 1) % count, i) for i in range(ends)])  8.75 us
  transfers between devices with their start and end apart: 17, of which 4 were waited for; matrix products, arithmetic and copies ran while one was open for 11% of the time, Pallas kernels for 0%

commit v1 on v0

v1 whole, which is shorter than its diff:
```python
import functools
import math

import jax
import jax.numpy as jnp
from jax import lax
from jax.experimental import pallas as pl
from jax.experimental.pallas import tpu as pltpu
from jax.sharding import PartitionSpec as P

MESH = pl.DeviceIdType.MESH

PLANES = 2
ZLO = 3
STEPS = 2
FREQ = 4
PML = 12
MATS = 4
TILE = 64

courant = 0.5
sigma_peak = 0.8
dft_weight = 0.5
sharpness = 4.0
threshold = 0.5
eps_low = 2.1
eps_high = 12.1
grad_scale = 0.01

F32 = jnp.float32
BF16 = jnp.bfloat16
VMEM = pl.BlockSpec(memory_space=pltpu.VMEM)
ANY = pl.BlockSpec(memory_space=pl.ANY)

CX, CY, NZ = 64, 256, 8
EX = CX + 8
KINDS = 8
EDGE = 2
ZL = KINDS * EDGE


def iota(shape, dim):
    return lax.broadcasted_iota(jnp.int32, shape, dim)


def wrapped(index, shift, count):
    return lax.rem(index + (shift + count), count)


def around(gx, gy, nx, ny):
    places = {}
    for dx in (-1, 0, 1):
        for dy in (-1, 0, 1):
            if dx or dy:
                places[dx, dy] = (wrapped(gx, dx, nx), wrapped(gy, dy, ny))
    return places


def remote(src, dst, send, recv, device):
    return pltpu.make_async_remote_copy(
        src_ref=src, dst_ref=dst, send_sem=send, recv_sem=recv, device_id=device, device_id_type=MESH
    )


def exchange_kernel(
    nx, ny,
    e_hbm, h_hbm, mat_hbm, den_hbm, fwd_hbm, adj_hbm,
    own, got, rim_prev, rim_next, xprev, xnext, total, gain,
    e, h, mat, den, fwd, adj, xdown, xup, load_sem, send_sem, recv_sem,
):
    gx, gy = lax.axis_index("gx"), lax.axis_index("gy")
    near = around(gx, gy, nx, ny)
    barrier = pltpu.get_barrier_semaphore()
    for device in near.values():
        pl.semaphore_signal(barrier, inc=1, device_id=device, device_id_type=MESH)

    loads = [
        pltpu.make_async_copy(src, dst, load_sem.at[i])
        for i, (src, dst) in enumerate(
            ((e_hbm, e), (h_hbm, h), (mat_hbm, mat), (den_hbm, den), (fwd_hbm, fwd), (adj_hbm, adj))
        )
    ]
    for load in loads:
        load.start()
    for load in loads[:4]:
        load.wait()

    lane = iota((CX, 128), 1)
    sub = iota((8, CY), 0)

    def plane(kind, z, rows, columns):
        if kind < 3:
            return e[kind, z, rows, columns]
        if kind < 6:
            return h[kind - 3, z, rows, columns]
        if kind == 6:
            return mat[z, rows, columns].astype(F32)
        return den[rows, columns]

    def pack(z, carry):
        first, last = carry
        every, low, high = pl.ds(0, CX), pl.ds(0, 128), pl.ds(128, 128)
        left = jnp.zeros((CX, 128), F32)
        right = jnp.zeros((CX, 128), F32)
        for kind in range(KINDS):
            mine = (lane >= EDGE * kind) & (lane < EDGE * (kind + 1))
            a = plane(kind, z, every, low)
            b = plane(kind, z, every, high)
            left = jnp.where(mine, pltpu.roll(a, EDGE * kind, 1) if kind else a, left)
            right = jnp.where(mine, pltpu.roll(b, EDGE * kind + EDGE, 1), right)
        first = first + pltpu.roll(left, z * ZL, 1)
        last = last + pltpu.roll(right, z * ZL, 1)
        for group in range(2):
            up = jnp.zeros((8, CY), F32)
            down = jnp.zeros((8, CY), F32)
            for q in range(4):
                kind = 4 * group + q
                mine = (sub >= 2 * q) & (sub < 2 * q + 2)
                a = plane(kind, z, pl.ds(0, 8), pl.ds(0, CY))
                b = plane(kind, z, pl.ds(CX - 8, 8), pl.ds(0, CY))
                up = jnp.where(mine, pltpu.roll(a, 2 * q, 0) if q else a, up)
                down = jnp.where(mine, pltpu.roll(b, 2 * q + 2, 0) if q < 3 else b, down)
            xup[2 * z + group] = up
            xdown[2 * z + group] = down
        return first, last

    empty = jnp.zeros((CX, 128), F32)
    first, last = lax.fori_loop(0, NZ, pack, (empty, empty))
    own[0] = first
    own[1] = last

    pl.semaphore_wait(barrier, 8)
    top, bottom = pl.ds(0, 8), pl.ds(CX - 8, 8)
    plan = (
        (own.at[1], got.at[0], (0, 1)),
        (own.at[0], got.at[1], (0, -1)),
        (xdown, xprev, (1, 0)),
        (xup, xnext, (-1, 0)),
        (own.at[:, bottom], rim_prev.at[pl.ds(1, 2)], (1, 0)),
        (own.at[:, top], rim_next.at[pl.ds(1, 2)], (-1, 0)),
        (own.at[1, bottom], rim_prev.at[0], (1, 1)),
        (own.at[0, bottom], rim_prev.at[3], (1, -1)),
        (own.at[1, top], rim_next.at[0], (-1, 1)),
        (own.at[0, top], rim_next.at[3], (-1, -1)),
    )
    copies = [
        remote(src, dst, send_sem.at[i], recv_sem.at[i], near[to]) for i, (src, dst, to) in enumerate(plan)
    ]
    for copy in copies:
        copy.start()

    for load in loads[4:]:
        load.wait()
    cosines = [[dft_weight * math.cos((0.21 + 0.06 * f) * (n + 1)) for f in range(FREQ)] for n in range(STEPS)]
    sines = [[dft_weight * math.sin((0.21 + 0.06 * f) * (n + 1)) for f in range(FREQ)] for n in range(STEPS)]

    def chunk(r, _):
        rows = pl.ds(pl.multiple_of(r * 16, 16), 16)

        def entry(k, acc):
            one = jnp.zeros((16, CY), F32)
            two = jnp.zeros((16, CY), F32)
            for f in range(FREQ):
                re = fwd[f, 0, k, rows].astype(F32)
                im = fwd[f, 1, k, rows].astype(F32)
                acc = acc + (re * adj[f, 0, k, rows] - im * adj[f, 1, k, rows])
                one = one + (cosines[0][f] * re + sines[0][f] * im)
                two = two + (cosines[1][f] * re + sines[1][f] * im)
            gain[k, 0, rows] = one
            gain[k, 1, rows] = two
            return acc

        total[rows] = lax.fori_loop(0, 3 * PLANES, entry, jnp.zeros((16, CY), F32))
        return 0

    lax.fori_loop(0, CX // 16, chunk, 0)
    for copy in copies:
        copy.wait()


def exchange(nx, ny, e, h, mat, den, fwd, adj):
    shape = jax.ShapeDtypeStruct
    return pl.pallas_call(
        functools.partial(exchange_kernel, nx, ny),
        name="exchange",
        out_shape=(
            shape((2, CX, 128), F32),
            shape((2, CX, 128), F32),
            shape((4, 8, 128), F32),
            shape((4, 8, 128), F32),
            shape((2 * NZ, 8, CY), F32),
            shape((2 * NZ, 8, CY), F32),
            shape((CX, CY), F32),
            shape((3 * PLANES, STEPS, CX, CY), F32),
        ),
        in_specs=[ANY] * 6,
        out_specs=(VMEM,) * 8,
        scratch_shapes=[
            pltpu.VMEM(e.shape, F32),
            pltpu.VMEM(h.shape, F32),
            pltpu.VMEM(mat.shape, jnp.int32),
            pltpu.VMEM(den.shape, F32),
            pltpu.VMEM(fwd.shape, BF16),
            pltpu.VMEM(adj.shape, F32),
            pltpu.VMEM((2 * NZ, 8, CY), F32),
            pltpu.VMEM((2 * NZ, 8, CY), F32),
            pltpu.SemaphoreType.DMA((6,)),
            pltpu.SemaphoreType.DMA((10,)),
            pltpu.SemaphoreType.DMA((10,)),
        ],
        compiler_params=pltpu.CompilerParams(collective_id=0, has_side_effects=True),
    )(e, h, mat, den, fwd, adj)


def profile(places, total):
    depth = jnp.maximum(jnp.maximum(PML - places, places - (total - 1 - PML)), 0.0) / PML
    return depth * depth * depth


def bend_of(filtered):
    return jnp.tanh(sharpness * (filtered - threshold))


def fdtd_kernel(
    nx, ny,
    e_ref, h_ref, mat_ref, den_ref, table_ref, own, got, rim_prev, rim_next, xprev, xnext, total, gain,
    e_out, h_out, local,
    E, H, CE, damp, ch, cm, slope, inter, strips,
):
    s = pl.program_id(0)
    gx, gy = lax.axis_index("gx"), lax.axis_index("gy")
    has_prev, has_next = gx > 0, gx < nx - 1
    has_left, has_right = gy > 0, gy < ny - 1
    total_x, total_y = nx * CX, ny * CY
    lane = iota((EX, 128), 1)
    half_sum_scale = math.tanh(sharpness * threshold) + math.tanh(sharpness * (1.0 - threshold))

    def xn(f):
        return pltpu.roll(f, EX - 1, 0)

    def xp(f):
        return pltpu.roll(f, 1, 0)

    def yn(f, strip, z):
        a, b = pltpu.roll(f[:, :128], 127, 1), pltpu.roll(f[:, 128:], 127, 1)
        edge = pltpu.roll(strip, 127 - 6 + 128 - z * ZL, 1)
        last = lane == 127
        return jnp.concatenate([jnp.where(last, b, a), jnp.where(last, edge, b)], axis=1)

    def yp(f, strip, z):
        a, b = pltpu.roll(f[:, :128], 1, 1), pltpu.roll(f[:, 128:], 1, 1)
        edge = pltpu.roll(strip, 127 - z * ZL, 1)
        first = lane == 0
        return jnp.concatenate([jnp.where(first, edge, a), jnp.where(first, a, b)], axis=1)

    def x_halo(kind, z):
        q = kind % 4
        sub = iota((8, CY), 0)
        ahead = xnext[2 * z + kind // 4]
        behind = xprev[2 * z + kind // 4]
        if q:
            ahead = pltpu.roll(ahead, 8 - 2 * q, 0)
        if q < 3:
            behind = pltpu.roll(behind, 6 - 2 * q, 0)
        return jnp.where((sub < 2) & has_next, ahead, jnp.where((sub >= 6) & has_prev, behind, 0.0))

    def places(columns, width):
        rows = iota((EX, width), 0)
        rows = gx * CX + jnp.where(rows < CX + 4, rows, rows - EX)
        inside = (rows >= 0) & (rows < total_x) & (columns >= 0) & (columns < total_y)
        sigma = sigma_peak * (profile(rows.astype(F32), total_x) + profile(columns.astype(F32), total_y))
        half = 1.0 + 0.5 * sigma
        damping = jnp.where(inside, (1.0 - 0.5 * sigma) / half, 0.0)
        return inside, half, damping, jnp.where(inside, courant / half, 0.0)

    def design(filtered):
        bend = bend_of(filtered)
        projected = (math.tanh(sharpness * threshold) + bend) / half_sum_scale
        return bend, eps_low + (eps_high - eps_low) * projected

    @pl.when(s == 0)
    def _():
        zero = jnp.zeros((EX, CY), F32)
        for c in range(3):
            E[c, NZ] = zero
            H[c, 0] = zero
        sub = iota((8, 128), 0)
        pieces = []
        for i, body in enumerate((got[0], own[0], own[1], got[1])):
            rim = jnp.where((sub < 4) & has_next, rim_next[i], jnp.where((sub >= 4) & has_prev, rim_prev[i], 0.0))
            piece = jnp.concatenate([body, rim], axis=0)
            if i == 0:
                piece = jnp.where(has_left, piece, 0.0)
            if i == 3:
                piece = jnp.where(has_right, piece, 0.0)
            pieces.append(piece)
        slot = lax.rem(lane, ZL)

        def strip(kind):
            value = jnp.zeros((EX, 128), F32)
            for i, piece in enumerate(pieces):
                shift = (EDGE * i - EDGE * kind) % 128
                moved = pltpu.roll(piece, shift, 1) if shift else piece
                value = jnp.where((slot >= EDGE * i) & (slot < EDGE * (i + 1)), moved, value)
            return value

        inside, half, damping, coef_h = places(gy * CY + iota((EX, CY), 1), CY)
        damp[...] = damping
        ch[...] = coef_h
        dens = jnp.concatenate([den_ref[...], x_halo(7, 0)], axis=0)
        dens_s = strip(7)
        sums = xp(dens) + 2.0 * dens + xn(dens)
        sums_s = xp(dens_s) + 2.0 * dens_s + xn(dens_s)
        filtered = (yp(sums, sums_s, ZLO) + 2.0 * sums + yn(sums, sums_s, ZLO)) / 16.0
        filtered_s = (pltpu.roll(sums_s, 1, 1) + 2.0 * sums_s + pltpu.roll(sums_s, 127, 1)) / 16.0
        bend, design_eps = design(filtered)
        slope[...] = (sharpness * (1.0 - bend * bend) / half_sum_scale)[:CX]
        for k in range(MATS):
            cm[k] = jnp.where(inside, courant / (table_ref[k] * half), 0.0)
        cm[MATS] = jnp.where(inside, courant / (design_eps * half), 0.0)
        inter[...] = total[...]

        columns = gy * CY + jnp.where(slot < 4, slot - EDGE, slot + (CY - EDGE - 4))
        inside, half, damping, coef_h = places(columns, 128)
        inside = inside & (slot < 8)
        damping = jnp.where(slot < 8, damping, 0.0)
        coef_h = jnp.where(slot < 8, coef_h, 0.0)
        mats = strip(6)
        eps = jnp.zeros((EX, 128), F32)
        for k in range(MATS):
            eps = jnp.where(mats == float(k), table_ref[k], eps)
        layer = (lane >= ZLO * ZL) & (lane < (ZLO + PLANES) * ZL)
        eps = jnp.where(layer, design(filtered_s)[1], eps)
        coef_e = jnp.where(inside, courant / (eps * half), 0.0)

        def yns(f):
            return pltpu.roll(f, 127, 1)

        def yps(f):
            return pltpu.roll(f, 1, 1)

        def zns(f):
            return jnp.where(lane < 128 - ZL, pltpu.roll(f, 128 - ZL, 1), 0.0)

        def zps(f):
            return jnp.where(lane >= ZL, pltpu.roll(f, ZL, 1), 0.0)

        def strip_h(ex, ey, ez, hx, hy, hz):
            cx = (yns(ez) - ez) - (zns(ey) - ey)
            cy = (zns(ex) - ex) - (xn(ez) - ez)
            cz = (xn(ey) - ey) - (yns(ex) - ex)
            return damping * hx - coef_h * cx, damping * hy - coef_h * cy, damping * hz - coef_h * cz

        def strip_e(ex, ey, ez, hx, hy, hz):
            cx = (hz - yps(hz)) - (hy - zps(hy))
            cy = (hx - zps(hx)) - (hz - xp(hz))
            cz = (hy - xp(hy)) - (hx - yps(hx))
            return damping * ex + coef_e * cx, damping * ey + coef_e * cy, damping * ez + coef_e * cz

        es = tuple(strip(c) for c in range(3))
        hs = tuple(strip(c) for c in range(3, 6))
        strips[0], strips[1] = es[0], es[2]
        hs = strip_h(*es, *hs)
        strips[2], strips[3] = hs[0], hs[2]
        es = strip_e(*es, *hs)
        strips[4], strips[5] = es[0], es[2]
        hs = strip_h(*es, *hs)
        strips[6], strips[7] = hs[0], hs[2]

    @pl.when(s < NZ)
    def _():
        for c in range(3):
            E[c, s] = jnp.concatenate([e_ref[c, 0], x_halo(c, s)], axis=0)
            H[c, s + 1] = jnp.concatenate([h_ref[c, 0], x_halo(3 + c, s)], axis=0)
        mats = jnp.concatenate([mat_ref[0].astype(F32), x_halo(6, s)], axis=0)
        mats = jnp.where((s >= ZLO) & (s < ZLO + PLANES), float(MATS), mats)
        coef = cm[MATS]
        for k in range(MATS):
            coef = jnp.where(mats == float(k), cm[k], coef)
        CE[s] = coef

    def half_h(z, first):
        ex, ey, ez = E[0, z], E[1, z], E[2, z]
        d, c = damp[...], ch[...]
        H[0, z + 1] = d * H[0, z + 1] - c * ((yn(ez, strips[first + 1], z) - ez) - (E[1, z + 1] - ey))
        H[1, z + 1] = d * H[1, z + 1] - c * ((E[0, z + 1] - ex) - (xn(ez) - ez))
        H[2, z + 1] = d * H[2, z + 1] - c * ((xn(ey) - ey) - (yn(ex, strips[first], z) - ex))

    def half_e(z, first):
        hx, hy, hz = H[0, z + 1], H[1, z + 1], H[2, z + 1]
        d, c = damp[...], CE[z]
        E[0, z] = d * E[0, z] + c * ((hz - yp(hz, strips[first + 1], z)) - (hy - H[1, z]))
        E[1, z] = d * E[1, z] + c * ((hx - H[0, z]) - (hz - xp(hz)))
        E[2, z] = d * E[2, z] + c * ((hy - xp(hy)) - (hx - yp(hx, strips[first], z)))

    def collect(z, n):
        @pl.when((z >= ZLO) & (z < ZLO + PLANES))
        def _():
            acc = inter[...]
            for c in range(3):
                acc = acc + gain[PLANES * c + (z - ZLO), n] * E[c, z, :CX]
            inter[...] = acc

    @pl.when((s >= 1) & (s <= NZ))
    def _():
        z = s - 1
        half_h(z, 0)
        half_e(z, 2)
        collect(z, 0)

    @pl.when(s >= 2)
    def _():
        z = s - 2
        half_h(z, 4)
        half_e(z, 6)
        collect(z, 1)
        for c in range(3):
            e_out[c, 0] = E[c, z, :CX]
            h_out[c, 0] = H[c, z + 1, :CX]

    @pl.when(s == NZ + 1)
    def _():
        local[...] = grad_scale * (eps_high - eps_low) * slope[...] * inter[...]


def fdtd(nx, ny, e, h, mat, den, table, halo):
    whole = lambda array: pl.BlockSpec(array.shape, lambda s: (0,) * array.ndim)
    incoming = pl.BlockSpec((3, 1, CX, CY), lambda s: (0, jnp.minimum(s, NZ - 1), 0, 0))
    outgoing = pl.BlockSpec((3, 1, CX, CY), lambda s: (0, jnp.maximum(s - 2, 0), 0, 0))
    shape = jax.ShapeDtypeStruct
    return pl.pallas_call(
        functools.partial(fdtd_kernel, nx, ny),
        name="fdtd",
        grid=(NZ + 2,),
        out_shape=(shape(e.shape, F32), shape(h.shape, F32), shape((CX, CY), F32)),
        in_specs=[
            incoming,
            incoming,
            pl.BlockSpec((1, CX, CY), lambda s: (jnp.minimum(s, NZ - 1), 0, 0)),
            whole(den),
            pl.BlockSpec(memory_space=pltpu.SMEM),
        ]
        + [whole(array) for array in halo],
        out_specs=(outgoing, outgoing, pl.BlockSpec((CX, CY), lambda s: (0, 0))),
        scratch_shapes=[
            pltpu.VMEM((3, NZ + 1, EX, CY), F32),
            pltpu.VMEM((3, NZ + 1, EX, CY), F32),
            pltpu.VMEM((NZ, EX, CY), F32),
            pltpu.VMEM((EX, CY), F32),
            pltpu.VMEM((EX, CY), F32),
            pltpu.VMEM((MATS + 1, EX, CY), F32),
            pltpu.VMEM((CX, CY), F32),
            pltpu.VMEM((CX, CY), F32),
            pltpu.VMEM((8, EX, 128), F32),
        ],
    )(e, h, mat, den, table, *halo)


def tiles_kernel(
    G, Zn,
    local, tile_map, out,
    rim_left, rim_right, rim_prev, rim_next, corner, cells, message, gathered, sums, arrived, ready, landed,
    rim_send, rim_recv, a_send, a_recv, b_send, b_recv, c_send, c_recv,
):
    gx, gy = lax.axis_index("gx"), lax.axis_index("gy")
    nx, ny = Zn * G, 2 * G
    x, core = gy // 2, lax.rem(gy, 2)
    z, y = gx // G, lax.rem(gx, G)

    def dev(x, y, z, core):
        return (z * G + y, x * 2 + core)

    near = around(gx, gy, nx, ny)
    partners = list(near.values())
    for k in range(1, G):
        for c in range(2):
            partners.append(dev(wrapped(x, k, G), y, z, c))
            partners.append(dev(x, wrapped(y, k, G), z, c))
    partners.append(dev(x, y, z, 1 - core))
    for k in range(1, Zn):
        for c in range(2):
            partners.append(dev(x, y, wrapped(z, k, Zn), c))
    barrier = pltpu.get_barrier_semaphore()
    for device in partners:
        pl.semaphore_signal(barrier, inc=1, device_id=device, device_id_type=MESH)
    pl.semaphore_wait(barrier, len(partners))

    low, high, top, bottom = pl.ds(0, 128), pl.ds(128, 128), pl.ds(0, 8), pl.ds(CX - 8, 8)
    plan = (
        (local.at[:, high], rim_left, (0, 1)),
        (local.at[:, low], rim_right, (0, -1)),
        (local.at[bottom], rim_prev, (1, 0)),
        (local.at[top], rim_next, (-1, 0)),
        (local.at[bottom, high], corner.at[0], (1, 1)),
        (local.at[bottom, low], corner.at[1], (1, -1)),
        (local.at[top, high], corner.at[2], (-1, 1)),
        (local.at[top, low], corner.at[3], (-1, -1)),
    )
    rims = [remote(src, dst, rim_send.at[i], rim_recv.at[i], near[to]) for i, (src, dst, to) in enumerate(plan)]
    for copy in rims:
        copy.start()

    lane8 = iota((8, 128), 1)
    names = jnp.zeros((8, 128), F32)
    for j in range(4):
        names = jnp.where(((lane8 == j) | (lane8 == 4 + j)), tile_map[0, j].astype(F32), names)
    message[0, pl.ds(CX, 8)] = names
    message[1, pl.ds(CX, 8)] = names

    for copy in rims:
        copy.wait_recv()

    lane = iota((EX, 128), 1)
    sub = iota((8, 128), 0)
    wide = iota((8, CY), 0)
    has_prev, has_next = gx > 0, gx < nx - 1
    has_left, has_right = gy > 0, gy < ny - 1
    rows = jnp.where((wide < 4) & has_next, rim_next[...], jnp.where((wide >= 4) & has_prev, rim_prev[...], 0.0))
    main = jnp.concatenate([local[...], rows], axis=0)
    left = jnp.concatenate(
        [
            rim_left[...],
            jnp.where((sub < 4) & has_next, corner[2], jnp.where((sub >= 4) & has_prev, corner[0], 0.0)),
        ],
        axis=0,
    )
    left = jnp.where(has_left, left, 0.0)
    right = jnp.concatenate(
        [
            rim_right[...],
            jnp.where((sub < 4) & has_next, corner[3], jnp.where((sub >= 4) & has_prev, corner[1], 0.0)),
        ],
        axis=0,
    )
    right = jnp.where(has_right, right, 0.0)

    def along_x(f):
        return pltpu.roll(f, 1, 0) + 2.0 * f + pltpu.roll(f, EX - 1, 0)

    a, b = along_x(main[:, :128]), along_x(main[:, 128:])
    left, right = along_x(left), along_x(right)
    first, last = lane == 0, lane == 127
    ra, rb = pltpu.roll(a, 1, 1), pltpu.roll(b, 1, 1)
    la, lb = pltpu.roll(a, 127, 1), pltpu.roll(b, 127, 1)
    left, right = pltpu.roll(left, 1, 1), pltpu.roll(right, 127, 1)
    a = (jnp.where(first, left, ra) + 2.0 * a + jnp.where(last, lb, la)) / 16.0
    b = (jnp.where(first, ra, rb) + 2.0 * b + jnp.where(last, right, lb)) / 16.0
    cells[0] = a[:CX]
    cells[1] = b[:CX]

    narrow = iota((CX // 2, 128), 1) < TILE
    for j in range(4):
        even = cells[j // 2, pl.ds(0, CX // 2, stride=2), :]
        odd = cells[j // 2, pl.ds(1, CX // 2, stride=2), :]
        if j % 2:
            tile = jnp.where(narrow, pltpu.roll(even, TILE, 1), odd)
        else:
            tile = jnp.where(narrow, even, pltpu.roll(odd, TILE, 1))
        for h in range(2):
            message[h, pl.ds(j, 16, stride=4), :] = tile[16 * h : 16 * h + 16]

    sends = []
    for k in range(1, G):
        sends.append((message.at[0], 2 * k + core, dev(wrapped(x, k, G), y, z, 0)))
        sends.append((message.at[1], 2 * k + core, dev(x, wrapped(y, k, G), z, 1)))
    sends.append((message.at[1 - core], core, dev(x, y, z, 1 - core)))
    first_stop = [
        remote(src, gathered.at[slot], a_send.at[i], a_recv.at[slot], to) for i, (src, slot, to) in enumerate(sends)
    ]
    for copy in first_stop:
        copy.start()
    gathered[core] = message[core]

    def arrival(slot):
        return remote(message.at[0], gathered.at[slot], a_send.at[0], a_recv.at[slot], dev(x, y, z, 1 - core))

    arrival(1 - core).wait_recv()
    for k in range(1, G):
        for c in range(2):
            arrival(2 * k + c).wait_recv()

    slots = 2 * G
    K = slots * 8
    P_rows = G * Zn * 2
    per = Zn * 2
    found = jnp.zeros((8, 128), F32)
    for slot in range(slots):
        part = gathered[slot, pl.ds(CX, 8)]
        part = pltpu.roll(part, 8 * slot, 1) if slot else part
        found = jnp.where((lane8 >= 8 * slot) & (lane8 < 8 * slot + 8), part, found)
    shift = K
    while shift < 128:
        found = jnp.where(lane8 < shift, found, pltpu.roll(found, shift, 1))
        shift *= 2
    found = jnp.broadcast_to(found[0:1], (2 * P_rows, 128))
    found = jnp.concatenate([found] * max(1, 4 * K // 128), axis=1)
    row = iota((2 * P_rows, 4 * K), 0)
    column = iota((2 * P_rows, 4 * K), 1)
    q = lax.rem(row // per, G)
    place = lax.rem(row, per)
    fixed = (1 - core) * (x * 2) + core * (y * (2 * G))
    param = (place // 2) * (2 * G * G) + lax.rem(place, 2) + q * ((1 - core) * (2 * G) + core * 2) + fixed
    same = (row // P_rows == lax.rem(column, 8) // 4) & (column < 3 * K)
    chosen = jnp.where(same & (found == param.astype(F32)), 1.0, 0.0).astype(BF16)

    for m in range(8):
        data = jnp.concatenate([gathered[slot, pl.ds(8 * m, 8)] for slot in range(slots)], axis=0)
        hi = data.astype(BF16)
        rest = data - hi.astype(F32)
        mid = rest.astype(BF16)
        lo = (rest - mid.astype(F32)).astype(BF16)
        picked = jnp.dot(chosen, jnp.concatenate([hi, mid, lo, hi], axis=0), preferred_element_type=F32)
        for parity in range(2):
            for place_q in range(G):
                start = parity * P_rows + place_q * per
                sums[place_q, 2 * m + parity] = picked[start : start + per]

    mine = (1 - core) * y + core * x
    second_stop = []
    for k in range(1, G):
        there = wrapped(mine, k, G)
        to = dev((1 - core) * x + core * there, (1 - core) * there + core * y, z, core)
        second_stop.append(remote(sums.at[there], arrived.at[k - 1], b_send.at[k - 1], b_recv.at[k - 1], to))
    for copy in second_stop:
        copy.start()
    for copy in second_stop:
        copy.wait_recv()
    for b in range(16):
        value = sums[mine, b]
        for k in range(G - 1):
            value = value + arrived[k, b]
        ready[pl.ds(b, per, stride=16), :] = value

    third_stop = []
    for k in range(Zn - 1, -1, -1):
        there = wrapped(z, k, Zn)
        for c in range(2):
            if k == 0 and c == 0:
                continue
            target = c if k else 1 - core
            start = pl.multiple_of((there * 2 + target) * 16, 16)
            i = 2 * k + c
            third_stop.append(
                remote(
                    ready.at[pl.ds(start, 16)], landed.at[2 * k + core], c_send.at[i], c_recv.at[2 * k + core],
                    dev(x, y, there, target),
                )
            )
    for copy in third_stop:
        copy.start()
    landed[core] = ready[pl.ds(pl.multiple_of((z * 2 + core) * 16, 16), 16)]

    def landing(slot):
        return remote(
            ready.at[pl.ds(0, 16)], landed.at[slot], c_send.at[0], c_recv.at[slot], dev(x, y, z, 1 - core)
        )

    landing(1 - core).wait_recv()
    for k in range(1, Zn):
        for c in range(2):
            landing(2 * k + c).wait_recv()
    for h in range(2):
        value = landed[h]
        for k in range(1, Zn):
            value = value + landed[2 * k + h]
        out[pl.ds(16 * h, 16)] = value
    for copy in rims + first_stop + second_stop + third_stop:
        copy.wait_send()


def route_tiles(G, Zn, local, tile_map):
    per = Zn * 2
    dma = pltpu.SemaphoreType.DMA
    return pl.pallas_call(
        functools.partial(tiles_kernel, G, Zn),
        name="tiles",
        out_shape=jax.ShapeDtypeStruct((32, 128), F32),
        in_specs=[VMEM, pl.BlockSpec(memory_space=pltpu.SMEM)],
        out_specs=VMEM,
        scratch_shapes=[
            pltpu.VMEM((CX, 128), F32),
            pltpu.VMEM((CX, 128), F32),
            pltpu.VMEM((8, CY), F32),
            pltpu.VMEM((8, CY), F32),
            pltpu.VMEM((4, 8, 128), F32),
            pltpu.VMEM((2, CX, 128), F32),
            pltpu.VMEM((2, CX + 8, 128), F32),
            pltpu.VMEM((2 * G, CX + 8, 128), F32),
            pltpu.VMEM((G, 16, per, 128), F32),
            pltpu.VMEM((G - 1, 16, per, 128), F32),
            pltpu.VMEM((per * 16, 128), F32),
            pltpu.VMEM((2 * Zn, 16, 128), F32),
            dma((8,)),
            dma((8,)),
            dma((2 * G,)),
            dma((2 * G,)),
            dma((G - 1,)),
            dma((G - 1,)),
            dma((2 * Zn,)),
            dma((2 * Zn,)),
        ],
        compiler_params=pltpu.CompilerParams(collective_id=1, has_side_effects=True),
    )(local, tile_map)


def on_device(nx, ny, e_adj, h_adj, density, material, eps_table, dft_adj, dft_fwd, tile_map):
    G = ny // 2
    flat = lambda array: array.reshape(FREQ, 2, 3 * PLANES, CX, CY)
    halo = exchange(nx, ny, e_adj, h_adj, material, density, flat(dft_fwd), flat(dft_adj))
    e_out, h_out, local = fdtd(nx, ny, e_adj, h_adj, material, density, eps_table, halo)
    params = route_tiles(G, nx // G, local, tile_map)
    return e_out, h_out, params.reshape(1, TILE * TILE)


def solution(mesh):
    in_specs = (
        P(None, None, "gx", "gy"),
        P(None, None, "gx", "gy"),
        P("gx", "gy"),
        P(None, "gx", "gy"),
        P(),
        P(None, None, None, None, "gx", "gy"),
        P(None, None, None, None, "gx", "gy"),
        P("gx", "gy"),
    )
    out_specs = (P(None, None, "gx", "gy"), P(None, None, "gx", "gy"), P(("gx", "gy"), None))
    return jax.shard_map(
        functools.partial(on_device, mesh.shape["gx"], mesh.shape["gy"]),
        mesh=mesh,
        in_specs=in_specs,
        out_specs=out_specs,
        check_vma=False,
    )
```

time: 435 us -> 57.6 us (0.13)
  waiting for transfers between devices: 279 us -> 0 us
  Pallas kernels: 0 us -> 55.3 us
  starting transfers between devices: 48 us -> 0 us
  local copies, waits for them, and re-layouts: 46.8 us -> 1.32 us
  other arithmetic: 40 us -> 0 us
  between operations: 14.9 us -> 0.65 us
    unnamed x2 -> x0, waiting for transfers between devices: 269 us -> none
    pallas_call x0 -> x3, Pallas kernels: none -> 55.3 us  [the longest x1 25.1 us: route_tiles(): pl.pallas_call(functools.partial(tiles_kernel, G, Zn), name='tiles', out_...]
    ppermute x16 -> x0, starting transfers between devices: 48 us -> none  [the longest x8 25.8 us: shifted(): return lax.ppermute(block, axis, route)]
    slice x42 -> x0, local copies, waits for them, and re-layouts: 29.7 us -> none  [the longest x12 12.8 us: step_next(): inner = lax.slice_in_dim(values, 1, values.shape[dim_index], axis=dim_index)]
    another operation x16 -> x0, other arithmetic: 15.2 us -> none  [the longest x4 12.9 us: on_device(): jnp.stack([elec_x, elec_y, elec_z])]
    add x8 -> x0, other arithmetic: 13.6 us -> none  [the longest x1 4.75 us: on_device(): elec_z = damping * elec_z + coef_e * curl_z]
    ppermute x16 -> x0, waiting for transfers between devices: 10.1 us -> none  [the longest x4 8.75 us: with_halo(): lax.ppermute(head, axis, [((i + 1) % count, i) for i in range(ends)])]
    sub x2 -> x0, other arithmetic: 8.14 us -> none  [on_device(): mag_x = damping * mag_x - coef_h * curl_x]
  transfers between devices with their start and end apart: 17 -> 0, of which waited for: 4 -> 0; matrix products, arithmetic and copies ran while one was open for 11% -> 0% of each run, Pallas kernels for 0% -> 0%
where the time goes in v1:
time: 57.6 us; the launch traced here: 57.3 us
  Pallas kernels  55.3 us (96%)
  local copies, waits for them, and re-layouts  1.32 us (2%)
  between operations  0.65 us (1%)
    pallas_call x1, Pallas kernels, route_tiles(): pl.pallas_call(functools.partial(tiles_kernel, G, Zn), name='tiles', out_...  25.1 us
    pallas_call x1, Pallas kernels, exchange(): pl.pallas_call(functools.partial(exchange_kernel, nx, ny), name='exchange...  19.6 us
    pallas_call x1, Pallas kernels, fdtd(): pl.pallas_call(functools.partial(fdtd_kernel, nx, ny), name='fdtd', grid=...  10.6 us
    unnamed x1, local copies, waits for them, and re-layouts  1.32 us

profile of v1, /device:TPU:1, one launch (start us, length us, event | category | flops | bytes accessed | tf_op | source)
XLA Modules:
  0.0 57.3 jit_solution(16045833154337492124)
XLA Ops:
  0.6 19.6 %exchange.1 = (f32[2,64,128]{2,1,0:T(8,128)}, f32[2,64,128]{2,1,0:T(8,128)}, f32[4,8,128]{2,1,0:T(8,128)}, f32[4,8,128]{2,1,0:T(8,128)}, f32[16,8,256]{2,1,0:T(8...) custom-call(f32[3,8,64,256]{3,2,1,0:T(8,128)} %e_ref.1, f32[3,8,64,256]{3,2,1,0:T(8,128)} %h_ref.1, ...), custom_call_target="tpu_custom_call" | custom-call | tf_op jit(solution)/shard_map/exchange/pallas_call | solution.py:183
  20.3 10.6 %fdtd.1 = (f32[3,8,64,256]{3,2,1,0:T(8,128)}, f32[3,8,64,256]{3,2,1,0:T(8,128)}, f32[64,256]{1,0:T(8,128)}) custom-call(f32[3,8,64,256]{3,2,1,0:T(8,128)} %e_ref.1, f32[3,8,64,256]{3,2,1,0:T(8,128)} %h_ref.1, s32[8,64,256]{2,1,0:T(8,128)} %mat_ref.1, f32[64,256]{1,0:T(8,128)} %den_ref.1, f32[4]{0:T(128)} %table_ref.1, f32[2,64,128]{2,1,0:T(8,128)} %get-tuple-element.14.own, ...), custom_call_target="tpu_custom_call" | custom-call | tf_op jit(solution)/shard_map/fdtd/pallas_call | solution.py:431
  30.9 25.1 %tiles.1 = f32[32,128]{1,0:T(8,128)} custom-call(f32[64,256]{1,0:T(8,128)} %get-tuple-element.24.local, s32[1,4]{1,0:T(1,128)} %tile_map.1), custom_call_target="tpu_custom_call" | custom-call | tf_op jit(solution)/shard_map/tiles/pallas_call | solution.py:674
  56.0 1.3 %copy.12 = f32[1,4096]{1,0:T(1,128)} copy(f32[1,4096]{1,0:T(1,128)} %bitcast.5) | data formatting | bytes 32768

commit v2 on v1

--- a/solution.py
+++ b/solution.py
@@ -459,8 +459,9 @@
 def tiles_kernel(
     G, Zn,
     local, tile_map, out,
-    rim_left, rim_right, rim_prev, rim_next, corner, cells, message, gathered, sums, arrived, ready, landed,
-    rim_send, rim_recv, a_send, a_recv, b_send, b_recv, c_send, c_recv,
+    rim_left, rim_right, rim_prev, rim_next, corner, cells, message, name_out, name_in, gathered, sums, passing, direct,
+    combined, ready, landed,
+    rim_send, rim_recv, name_send, name_recv, a_send, a_recv, b_send, b_recv, c_send, c_recv, heard,
 ):
     gx, gy = lax.axis_index("gx"), lax.axis_index("gy")
     nx, ny = Zn * G, 2 * G
@@ -469,6 +470,9 @@
 
     def dev(x, y, z, core):
         return (z * G + y, x * 2 + core)
+
+    def signal(semaphore, device):
+        pl.semaphore_signal(semaphore, inc=1, device_id=device, device_id_type=MESH)
 
     near = around(gx, gy, nx, ny)
     partners = list(near.values())
@@ -477,38 +481,103 @@
             partners.append(dev(wrapped(x, k, G), y, z, c))
             partners.append(dev(x, wrapped(y, k, G), z, c))
     partners.append(dev(x, y, z, 1 - core))
-    for k in range(1, Zn):
-        for c in range(2):
-            partners.append(dev(x, y, wrapped(z, k, Zn), c))
+    above, below = wrapped(z, 1, Zn), wrapped(z, -1, Zn)
+    for c in range(2):
+        partners.append(dev(x, y, above, c))
+        partners.append(dev(x, y, below, c))
     barrier = pltpu.get_barrier_semaphore()
     for device in partners:
-        pl.semaphore_signal(barrier, inc=1, device_id=device, device_id_type=MESH)
+        signal(barrier, device)
+    names = jnp.zeros((8, 128), F32)
+    lane8 = iota((8, 128), 1)
+    for j in range(4):
+        names = jnp.where(((lane8 == j) | (lane8 == 4 + j)), tile_map[0, j].astype(F32), names)
+    name_out[...] = names
     pl.semaphore_wait(barrier, len(partners))
+
+    rounds = Zn // 2 - 1
+
+    def pass_word(i):
+        if i < rounds:
+            signal(heard.at[i], dev(x, y, above, core))
+            signal(heard.at[i], dev(x, y, below, core))
+
+    def hear_word(i):
+        if i < rounds:
+            pl.semaphore_wait(heard.at[i], 2)
 
     low, high, top, bottom = pl.ds(0, 128), pl.ds(128, 128), pl.ds(0, 8), pl.ds(CX - 8, 8)
     plan = (
-        (local.at[:, high], rim_left, (0, 1)),
-        (local.at[:, low], rim_right, (0, -1)),
-        (local.at[bottom], rim_prev, (1, 0)),
-        (local.at[top], rim_next, (-1, 0)),
         (local.at[bottom, high], corner.at[0], (1, 1)),
         (local.at[bottom, low], corner.at[1], (1, -1)),
         (local.at[top, high], corner.at[2], (-1, 1)),
         (local.at[top, low], corner.at[3], (-1, -1)),
+        (local.at[bottom], rim_prev, (1, 0)),
+        (local.at[top], rim_next, (-1, 0)),
+        (local.at[:, high], rim_left, (0, 1)),
+        (local.at[:, low], rim_right, (0, -1)),
     )
     rims = [remote(src, dst, rim_send.at[i], rim_recv.at[i], near[to]) for i, (src, dst, to) in enumerate(plan)]
     for copy in rims:
         copy.start()
-
-    lane8 = iota((8, 128), 1)
-    names = jnp.zeros((8, 128), F32)
-    for j in range(4):
-        names = jnp.where(((lane8 == j) | (lane8 == 4 + j)), tile_map[0, j].astype(F32), names)
-    message[0, pl.ds(CX, 8)] = names
-    message[1, pl.ds(CX, 8)] = names
+    pass_word(0)
+
+    targets = []
+    for k in (2, 1, 3) if G == 4 else range(1, G):
+        targets.append((0, 2 * k + core, dev(wrapped(x, k, G), y, z, 0)))
+        targets.append((1, 2 * k + core, dev(x, wrapped(y, k, G), z, 1)))
+    targets.append((1 - core, core, dev(x, y, z, 1 - core)))
+    other = dev(x, y, z, 1 - core)
+    slots = 2 * G
+    name_copies = [
+        remote(name_out, name_in.at[slot], name_send.at[i], name_recv.at[slot], to)
+        for i, (_, slot, to) in enumerate(targets)
+    ]
+    for copy in name_copies:
+        copy.start()
+    name_in[core] = name_out[...]
+
+    def each_slot(wait):
+        wait(1 - core)
+        for k in range(1, G):
+            for c in range(2):
+                wait(2 * k + c)
+
+    each_slot(lambda slot: remote(name_out, name_in.at[slot], name_send.at[0], name_recv.at[slot], other).wait_recv())
+
+    K = slots * 8
+    P_rows = G * Zn * 2
+    per = Zn * 2
+    found = jnp.zeros((8, 128), F32)
+    for slot in range(slots):
+        part = name_in[slot]
+        part = pltpu.roll(part, 8 * slot, 1) if slot else part
+        found = jnp.where((lane8 >= 8 * slot) & (lane8 < 8 * slot + 8), part, found)
+    shift = K
+    while shift < 128:
+        found = jnp.where(lane8 < shift, found, pltpu.roll(found, shift, 1))
+        shift *= 2
+    found = jnp.broadcast_to(found[0:1], (P_rows, 128))
+    row = iota((P_rows, 128), 0)
+    column = iota((P_rows, 128), 1)
+    q = row // per
+    place = lax.rem(row, per)
+    fixed = (1 - core) * (x * 2) + core * (y * (2 * G))
+    param = (place // 2) * (2 * G * G) + lax.rem(place, 2) + q * ((1 - core) * (2 * G) + core * 2) + fixed
+    match = found == param.astype(F32)
+    even_cells = lax.rem(column, 8) < 4
+    both = jnp.concatenate(
+        [jnp.where(match & even_cells, 1.0, 0.0), jnp.where(match & (~even_cells), 1.0, 0.0)], axis=0
+    )
+    half_k = jnp.where(iota((2 * P_rows, 128), 1) < max(0, 3 * K - 128), both, 0.0)
+    chosen = jnp.concatenate([both, half_k], axis=1).astype(BF16) if K == 64 else jnp.where(
+        iota((2 * P_rows, 128), 1) < 3 * K, both, 0.0
+    ).astype(BF16)
 
     for copy in rims:
         copy.wait_recv()
+    hear_word(0)
+    pass_word(1)
 
     lane = iota((EX, 128), 1)
     sub = iota((8, 128), 0)
@@ -559,112 +628,107 @@
         for h in range(2):
             message[h, pl.ds(j, 16, stride=4), :] = tile[16 * h : 16 * h + 16]
 
-    sends = []
-    for k in range(1, G):
-        sends.append((message.at[0], 2 * k + core, dev(wrapped(x, k, G), y, z, 0)))
-        sends.append((message.at[1], 2 * k + core, dev(x, wrapped(y, k, G), z, 1)))
-    sends.append((message.at[1 - core], core, dev(x, y, z, 1 - core)))
-    first_stop = [
-        remote(src, gathered.at[slot], a_send.at[i], a_recv.at[slot], to) for i, (src, slot, to) in enumerate(sends)
-    ]
-    for copy in first_stop:
+    chunk_rows = [pl.ds(32 * ch, 32) for ch in range(2)]
+    first_stop = []
+    for ch in range(2):
+        for i, (h, slot, to) in enumerate(targets):
+            copy = remote(
+                message.at[h, chunk_rows[ch]], gathered.at[slot, chunk_rows[ch]], a_send.at[ch, i], a_recv.at[ch, slot], to
+            )
+            copy.start()
+            first_stop.append(copy)
+    gathered[core] = message[core]
+
+    mine = (1 - core) * y + core * x
+
+    def ring(k):
+        there = wrapped(mine, k, G)
+        return there, dev((1 - core) * x + core * there, (1 - core) * there + core * y, z, core)
+
+    ahead, to_ahead = ring(1)
+    behind, to_behind = ring(-1)
+    across, _ = ring(2)
+    second_stop = []
+    for ch in range(2):
+        each_slot(
+            lambda slot: remote(
+                message.at[0, chunk_rows[ch]], gathered.at[slot, chunk_rows[ch]], a_send.at[ch, 0], a_recv.at[ch, slot], other
+            ).wait_recv()
+        )
+        for m in range(4 * ch, 4 * ch + 4):
+            data = jnp.concatenate([gathered[slot, pl.ds(8 * m, 8)] for slot in range(slots)], axis=0)
+            hi = data.astype(BF16)
+            rest = data - hi.astype(F32)
+            mid = rest.astype(BF16)
+            lo = (rest - mid.astype(F32)).astype(BF16)
+            picked = jnp.dot(chosen, jnp.concatenate([hi, mid, lo, hi], axis=0), preferred_element_type=F32)
+            for parity in range(2):
+                for place_q in range(G):
+                    start = parity * P_rows + place_q * per
+                    sums[ch, place_q, 2 * (m - 4 * ch) + parity] = picked[start : start + per]
+        far, near_by = (to_ahead, to_behind) if ch == 0 else (to_behind, to_ahead)
+        straight = behind if ch == 0 else ahead
+        second_stop.append(remote(sums.at[ch, across], passing.at[ch], b_send.at[ch, 0], b_recv.at[ch, 0], far))
+        second_stop.append(remote(sums.at[ch, straight], direct.at[ch], b_send.at[ch, 1], b_recv.at[ch, 1], near_by))
+        second_stop[-2].start()
+        second_stop[-1].start()
+    hear_word(1)
+    pass_word(2)
+    for ch in range(2):
+        far = to_ahead if ch == 0 else to_behind
+        onward = ahead if ch == 0 else behind
+        second_stop[2 * ch].wait_recv()
+        passing[ch] = passing[ch] + sums[ch, onward]
+        copy = remote(passing.at[ch], combined.at[ch], b_send.at[ch, 2], b_recv.at[ch, 2], far)
         copy.start()
-    gathered[core] = message[core]
-
-    def arrival(slot):
-        return remote(message.at[0], gathered.at[slot], a_send.at[0], a_recv.at[slot], dev(x, y, z, 1 - core))
-
-    arrival(1 - core).wait_recv()
-    for k in range(1, G):
-        for c in range(2):
-            arrival(2 * k + c).wait_recv()
-
-    slots = 2 * G
-    K = slots * 8
-    P_rows = G * Zn * 2
-    per = Zn * 2
-    found = jnp.zeros((8, 128), F32)
-    for slot in range(slots):
-        part = gathered[slot, pl.ds(CX, 8)]
-        part = pltpu.roll(part, 8 * slot, 1) if slot else part
-        found = jnp.where((lane8 >= 8 * slot) & (lane8 < 8 * slot + 8), part, found)
-    shift = K
-    while shift < 128:
-        found = jnp.where(lane8 < shift, found, pltpu.roll(found, shift, 1))
-        shift *= 2
-    found = jnp.broadcast_to(found[0:1], (2 * P_rows, 128))
-    found = jnp.concatenate([found] * max(1, 4 * K // 128), axis=1)
-    row = iota((2 * P_rows, 4 * K), 0)
-    column = iota((2 * P_rows, 4 * K), 1)
-    q = lax.rem(row // per, G)
-    place = lax.rem(row, per)
-    fixed = (1 - core) * (x * 2) + core * (y * (2 * G))
-    param = (place // 2) * (2 * G * G) + lax.rem(place, 2) + q * ((1 - core) * (2 * G) + core * 2) + fixed
-    same = (row // P_rows == lax.rem(column, 8) // 4) & (column < 3 * K)
-    chosen = jnp.where(same & (found == param.astype(F32)), 1.0, 0.0).astype(BF16)
-
-    for m in range(8):
-        data = jnp.concatenate([gathered[slot, pl.ds(8 * m, 8)] for slot in range(slots)], axis=0)
-        hi = data.astype(BF16)
-        rest = data - hi.astype(F32)
-        mid = rest.astype(BF16)
-        lo = (rest - mid.astype(F32)).astype(BF16)
-        picked = jnp.dot(chosen, jnp.concatenate([hi, mid, lo, hi], axis=0), preferred_element_type=F32)
-        for parity in range(2):
-            for place_q in range(G):
-                start = parity * P_rows + place_q * per
-                sums[place_q, 2 * m + parity] = picked[start : start + per]
-
-    mine = (1 - core) * y + core * x
-    second_stop = []
-    for k in range(1, G):
-        there = wrapped(mine, k, G)
-        to = dev((1 - core) * x + core * there, (1 - core) * there + core * y, z, core)
-        second_stop.append(remote(sums.at[there], arrived.at[k - 1], b_send.at[k - 1], b_recv.at[k - 1], to))
-    for copy in second_stop:
-        copy.start()
-    for copy in second_stop:
-        copy.wait_recv()
-    for b in range(16):
-        value = sums[mine, b]
-        for k in range(G - 1):
-            value = value + arrived[k, b]
-        ready[pl.ds(b, per, stride=16), :] = value
+        second_stop.append(copy)
+    hear_word(2)
 
     third_stop = []
-    for k in range(Zn - 1, -1, -1):
-        there = wrapped(z, k, Zn)
-        for c in range(2):
-            if k == 0 and c == 0:
-                continue
-            target = c if k else 1 - core
-            start = pl.multiple_of((there * 2 + target) * 16, 16)
-            i = 2 * k + c
-            third_stop.append(
-                remote(
-                    ready.at[pl.ds(start, 16)], landed.at[2 * k + core], c_send.at[i], c_recv.at[2 * k + core],
+    for ch in range(2):
+        second_stop[2 * ch + 1].wait_recv()
+        second_stop[4 + ch].wait_recv()
+        for b in range(8):
+            value = sums[ch, mine, b] + direct[ch, b] + combined[ch, b]
+            ready[ch, pl.ds(b, per, stride=8), :] = value
+        eight = pl.ds(8 * ch, 8)
+        order = sorted(range(Zn), key=lambda k: -min(k, Zn - k))
+        for k in order:
+            there = wrapped(z, k, Zn)
+            for c in range(2):
+                if k == 0 and c == 0:
+                    continue
+                target = c if k else 1 - core
+                start = pl.multiple_of((there * 2 + target) * 8, 8)
+                copy = remote(
+                    ready.at[ch, pl.ds(start, 8)],
+                    landed.at[2 * k + core, eight],
+                    c_send.at[ch, 2 * k + c],
+                    c_recv.at[ch, 2 * k + core],
                     dev(x, y, there, target),
                 )
-            )
-    for copy in third_stop:
-        copy.start()
-    landed[core] = ready[pl.ds(pl.multiple_of((z * 2 + core) * 16, 16), 16)]
-
-    def landing(slot):
-        return remote(
-            ready.at[pl.ds(0, 16)], landed.at[slot], c_send.at[0], c_recv.at[slot], dev(x, y, z, 1 - core)
-        )
-
-    landing(1 - core).wait_recv()
-    for k in range(1, Zn):
-        for c in range(2):
-            landing(2 * k + c).wait_recv()
-    for h in range(2):
-        value = landed[h]
+                copy.start()
+                third_stop.append(copy)
+        landed[core, eight] = ready[ch, pl.ds(pl.multiple_of((z * 2 + core) * 8, 8), 8)]
+
+    for ch in range(2):
+        eight = pl.ds(8 * ch, 8)
+
+        def landing(slot):
+            remote(
+                ready.at[ch, pl.ds(0, 8)], landed.at[slot, eight], c_send.at[ch, 0], c_recv.at[ch, slot], other
+            ).wait_recv()
+
+        landing(1 - core)
         for k in range(1, Zn):
-            value = value + landed[2 * k + h]
-        out[pl.ds(16 * h, 16)] = value
-    for copy in rims + first_stop + second_stop + third_stop:
+            for c in range(2):
+                landing(2 * k + c)
+        for h in range(2):
+            value = landed[h, eight]
+            for k in range(1, Zn):
+                value = value + landed[2 * k + h, eight]
+            out[pl.ds(16 * h + 8 * ch, 8)] = value
+    for copy in rims + name_copies + first_stop + second_stop + third_stop:
         copy.wait_send()
 
 
@@ -684,20 +748,27 @@
             pltpu.VMEM((8, CY), F32),
             pltpu.VMEM((4, 8, 128), F32),
             pltpu.VMEM((2, CX, 128), F32),
-            pltpu.VMEM((2, CX + 8, 128), F32),
-            pltpu.VMEM((2 * G, CX + 8, 128), F32),
-            pltpu.VMEM((G, 16, per, 128), F32),
-            pltpu.VMEM((G - 1, 16, per, 128), F32),
-            pltpu.VMEM((per * 16, 128), F32),
+            pltpu.VMEM((2, CX, 128), F32),
+            pltpu.VMEM((8, 128), F32),
+            pltpu.VMEM((2 * G, 8, 128), F32),
+            pltpu.VMEM((2 * G, CX, 128), F32),
+            pltpu.VMEM((2, G, 8, per, 128), F32),
+            pltpu.VMEM((2, 8, per, 128), F32),
+            pltpu.VMEM((2, 8, per, 128), F32),
+            pltpu.VMEM((2, 8, per, 128), F32),
+            pltpu.VMEM((2, per * 8, 128), F32),
             pltpu.VMEM((2 * Zn, 16, 128), F32),
             dma((8,)),
             dma((8,)),
             dma((2 * G,)),
             dma((2 * G,)),
-            dma((G - 1,)),
-            dma((G - 1,)),
-            dma((2 * Zn,)),
-            dma((2 * Zn,)),
+            dma((2, 2 * G)),
+            dma((2, 2 * G)),
+            dma((2, 3)),
+            dma((2, 3)),
+            dma((2, 2 * Zn)),
+            dma((2, 2 * Zn)),
+            pltpu.SemaphoreType.REGULAR((3,)),
         ],
         compiler_params=pltpu.CompilerParams(collective_id=1, has_side_effects=True),
     )(local, tile_map)

time: 57.6 us -> 57.6 us (level)
  no operation moved by 1% of the time
where the time goes in v2:
time: 57.6 us; the launch traced here: 57.3 us
  Pallas kernels  55.3 us (96%)
  local copies, waits for them, and re-layouts  1.32 us (2%)
  between operations  0.65 us (1%)
    pallas_call x1, Pallas kernels, route_tiles(): pl.pallas_call(functools.partial(tiles_kernel, G, Zn), name='tiles', out_...  25 us
    pallas_call x1, Pallas kernels, exchange(): pl.pallas_call(functools.partial(exchange_kernel, nx, ny), name='exchange...  19.6 us
    pallas_call x1, Pallas kernels, fdtd(): pl.pallas_call(functools.partial(fdtd_kernel, nx, ny), name='fdtd', grid=...  10.6 us
    unnamed x1, local copies, waits for them, and re-layouts  1.32 us

profile of v2, /device:TPU:1, one launch (start us, length us, event | category | flops | bytes accessed | tf_op | source)
XLA Modules:
  0.0 57.3 jit_solution(5807951510479562462)
XLA Ops:
  0.6 19.6 %exchange.1 = (f32[2,64,128]{2,1,0:T(8,128)}, f32[2,64,128]{2,1,0:T(8,128)}, f32[4,8,128]{2,1,0:T(8,128)}, f32[4,8,128]{2,1,0:T(8,128)}, f32[16,8,256]{2,1,0:T(8...) custom-call(f32[3,8,64,256]{3,2,1,0:T(8,128)} %e_ref.1, f32[3,8,64,256]{3,2,1,0:T(8,128)} %h_ref.1, ...), custom_call_target="tpu_custom_call" | custom-call | tf_op jit(solution)/shard_map/exchange/pallas_call | solution.py:183
  20.3 10.6 %fdtd.1 = (f32[3,8,64,256]{3,2,1,0:T(8,128)}, f32[3,8,64,256]{3,2,1,0:T(8,128)}, f32[64,256]{1,0:T(8,128)}) custom-call(f32[3,8,64,256]{3,2,1,0:T(8,128)} %e_ref.1, f32[3,8,64,256]{3,2,1,0:T(8,128)} %h_ref.1, s32[8,64,256]{2,1,0:T(8,128)} %mat_ref.1, f32[64,256]{1,0:T(8,128)} %den_ref.1, f32[4]{0:T(128)} %table_ref.1, f32[2,64,128]{2,1,0:T(8,128)} %get-tuple-element.14.own, ...), custom_call_target="tpu_custom_call" | custom-call | tf_op jit(solution)/shard_map/fdtd/pallas_call | solution.py:431
  30.9 25.0 %tiles.1 = f32[32,128]{1,0:T(8,128)} custom-call(f32[64,256]{1,0:T(8,128)} %get-tuple-element.24.local, s32[1,4]{1,0:T(1,128)} %tile_map.1), custom_call_target="tpu_custom_call" | custom-call | tf_op jit(solution)/shard_map/tiles/pallas_call | solution.py:738
  55.9 1.3 %copy.12 = f32[1,4096]{1,0:T(1,128)} copy(f32[1,4096]{1,0:T(1,128)} %bitcast.5) | data formatting | bytes 32768

commit v3 on v0

v3 whole, which is shorter than its diff:
```python
import functools
import math

import jax
import jax.numpy as jnp
from jax import lax
from jax.experimental import pallas as pl
from jax.experimental.pallas import tpu as pltpu
from jax.sharding import PartitionSpec as P

MESH = pl.DeviceIdType.MESH

PLANES = 2
ZLO = 3
STEPS = 2
FREQ = 4
PML = 12
MATS = 4
TILE = 64

courant = 0.5
sigma_peak = 0.8
dft_weight = 0.5
sharpness = 4.0
threshold = 0.5
eps_low = 2.1
eps_high = 12.1
grad_scale = 0.01

F32 = jnp.float32
BF16 = jnp.bfloat16
VMEM = pl.BlockSpec(memory_space=pltpu.VMEM)
ANY = pl.BlockSpec(memory_space=pl.ANY)

CX, CY, NZ = 64, 256, 8
EX = CX + 8
KINDS = 8
EDGE = 2
ZL = KINDS * EDGE


def iota(shape, dim):
    return lax.broadcasted_iota(jnp.int32, shape, dim)


def wrapped(index, shift, count):
    return lax.rem(index + (shift + count), count)


def around(gx, gy, nx, ny):
    places = {}
    for dx in (-1, 0, 1):
        for dy in (-1, 0, 1):
            if dx or dy:
                places[dx, dy] = (wrapped(gx, dx, nx), wrapped(gy, dy, ny))
    return places


def remote(src, dst, send, recv, device):
    return pltpu.make_async_remote_copy(
        src_ref=src, dst_ref=dst, send_sem=send, recv_sem=recv, device_id=device, device_id_type=MESH
    )


def profile(places, total):
    depth = jnp.maximum(jnp.maximum(PML - places, places - (total - 1 - PML)), 0.0) / PML
    return depth * depth * depth


DOWN_GROUPS = NZ + (NZ * 6 + 7) // 8
UP_GROUPS = NZ + (NZ * 3 + 7) // 8


def row_slot(down, kind, z):
    if kind < 3:
        return z, 2 * kind, 2
    if kind == 6:
        return z, 6, 1
    each = 2 if down else 1
    row = (3 * z + kind - 3) * each
    return NZ + row // 8, row % 8, each


def solve_kernel(
    G, Zn,
    e_hbm, h_hbm, mat_hbm, den_hbm, fwd_hbm, adj_hbm, table_ref, tile_map,
    e_out, h_out, out,
    E, H, CE, mat, den, fwd, adj, gain, inter, slope, damp, coef, own, got, halo_prev, halo_next, xdown, xup, xprev, xnext, strips,
    local, rim_left, rim_right, rim_prev, rim_next, corner, cells, message, name_out, name_in, gathered, sums, passing, direct,
    combined, ready, landed,
    load_sem, halo_send, halo_recv,
    rim_send, rim_recv, name_send, name_recv, a_send, a_recv, b_send, b_recv, c_send, c_recv, heard,
):
    gx, gy = lax.axis_index("gx"), lax.axis_index("gy")
    nx, ny = Zn * G, 2 * G
    x, core = gy // 2, lax.rem(gy, 2)
    z, y = gx // G, lax.rem(gx, G)
    has_prev, has_next = gx > 0, gx < nx - 1
    has_left, has_right = gy > 0, gy < ny - 1
    total_x, total_y = nx * CX, ny * CY

    def dev(x, y, z, core):
        return (z * G + y, x * 2 + core)

    def signal(semaphore, device):
        pl.semaphore_signal(semaphore, inc=1, device_id=device, device_id_type=MESH)

    near = around(gx, gy, nx, ny)
    partners = list(near.values())
    for k in range(1, G):
        for c in range(2):
            partners.append(dev(wrapped(x, k, G), y, z, c))
            partners.append(dev(x, wrapped(y, k, G), z, c))
    partners.append(dev(x, y, z, 1 - core))
    above, below = wrapped(z, 1, Zn), wrapped(z, -1, Zn)
    for c in range(2):
        partners.append(dev(x, y, above, c))
        partners.append(dev(x, y, below, c))
    barrier = pltpu.get_barrier_semaphore()
    for device in partners:
        signal(barrier, device)

    block = pl.ds(0, CX)
    loads = []

    def load(src, dst):
        copy = pltpu.make_async_copy(src, dst, load_sem.at[len(loads)])
        copy.start()
        loads.append(copy)
        return copy

    load_den = load(den_hbm, den)
    load_mat = load(mat_hbm, mat)
    load_planes = [
        (load(e_hbm.at[:, p], E.at[:, p, block]), load(h_hbm.at[:, p], H.at[:, p + 1, block])) for p in range(NZ)
    ]
    load_dft = [load(fwd_hbm, fwd), load(adj_hbm, adj)]

    names = jnp.zeros((8, 128), F32)
    lane8 = iota((8, 128), 1)
    for j in range(4):
        names = jnp.where(((lane8 == j) | (lane8 == 4 + j)), tile_map[0, j].astype(F32), names)
    name_out[...] = names

    lane64 = iota((CX, 128), 1)
    low, high, top, bottom = pl.ds(0, 128), pl.ds(128, 128), pl.ds(0, 8), pl.ds(CX - 8, 8)

    def plane(kind, p, rows, columns):
        if kind < 3:
            return E[kind, p, rows, columns]
        if kind < 6:
            return H[kind - 3, p + 1, rows, columns]
        if kind == 6:
            return mat[p, rows, columns].astype(F32)
        return den[rows, columns]

    load_den.wait()
    load_mat.wait()
    first = jnp.zeros((CX, 128), F32)
    last = jnp.zeros((CX, 128), F32)
    empty = jnp.zeros((8, CY), F32)
    for g in range(DOWN_GROUPS - 1, DOWN_GROUPS):
        xdown[g] = empty
    for g in range(UP_GROUPS):
        xup[g] = empty
    for p in range(NZ):
        for copy in load_planes[p]:
            copy.wait()
        kinds = list(range(7)) + ([7] if ZLO <= p < ZLO + PLANES else [])
        for kind in kinds:
            at = p * ZL + EDGE * kind
            mine = (lane64 >= at) & (lane64 < at + EDGE)
            a = plane(kind, p, block, low)
            b = plane(kind, p, block, high)
            first = jnp.where(mine, pltpu.roll(a, at, 1) if at else a, first)
            last = jnp.where(mine, pltpu.roll(b, at + EDGE, 1) if at + EDGE < 128 else b, last)
        for kind in range(7):
            g, row, n = row_slot(True, kind, p)
            xdown[g, pl.ds(row, n)] = plane(kind, p, pl.ds(CX - n, n), pl.ds(0, CY))
            g, row, n = row_slot(False, kind, p)
            xup[g, pl.ds(row, n)] = plane(kind, p, pl.ds(0, n), pl.ds(0, CY))
        xdown[p, pl.ds(7, 1)] = den[pl.ds(CX - 2 + p % 2, 1), :]
        xup[p, pl.ds(7, 1)] = den[pl.ds(p % 2, 1), :]
    own[0] = first
    own[1] = last

    pl.semaphore_wait(barrier, len(partners))

    rounds = Zn // 2 - 1

    def pass_word(i):
        if i < rounds:
            signal(heard.at[i], dev(x, y, above, core))
            signal(heard.at[i], dev(x, y, below, core))

    def hear_word(i):
        if i < rounds:
            pl.semaphore_wait(heard.at[i], 2)

    plan = (
        (xdown, xprev, (1, 0)),
        (xup, xnext, (-1, 0)),
        (own.at[1], got.at[0], (0, 1)),
        (own.at[0], got.at[1], (0, -1)),
        (own.at[:, bottom], halo_prev.at[pl.ds(1, 2)], (1, 0)),
        (own.at[:, top], halo_next.at[pl.ds(1, 2)], (-1, 0)),
        (own.at[1, bottom], halo_prev.at[0], (1, 1)),
        (own.at[0, bottom], halo_prev.at[3], (1, -1)),
        (own.at[1, top], halo_next.at[0], (-1, 1)),
        (own.at[0, top], halo_next.at[3], (-1, -1)),
    )
    halos = [remote(src, dst, halo_send.at[i], halo_recv.at[i], near[to]) for i, (src, dst, to) in enumerate(plan)]
    for copy in halos:
        copy.start()
    pass_word(0)

    targets = []
    for k in (2, 1, 3) if G == 4 else range(1, G):
        targets.append((0, 2 * k + core, dev(wrapped(x, k, G), y, z, 0)))
        targets.append((1, 2 * k + core, dev(x, wrapped(y, k, G), z, 1)))
    targets.append((1 - core, core, dev(x, y, z, 1 - core)))
    other = dev(x, y, z, 1 - core)
    slots = 2 * G
    name_copies = [
        remote(name_out, name_in.at[slot], name_send.at[i], name_recv.at[slot], to)
        for i, (_, slot, to) in enumerate(targets)
    ]
    for copy in name_copies:
        copy.start()
    name_in[core] = name_out[...]

    def each_slot(wait):
        wait(1 - core)
        for k in range(1, G):
            for c in range(2):
                wait(2 * k + c)

    for copy in load_dft:
        copy.wait()
    cosines = [[dft_weight * math.cos((0.21 + 0.06 * f) * (n + 1)) for f in range(FREQ)] for n in range(STEPS)]
    sines = [[dft_weight * math.sin((0.21 + 0.06 * f) * (n + 1)) for f in range(FREQ)] for n in range(STEPS)]

    def chunk(r, _):
        rows = pl.ds(pl.multiple_of(r * 16, 16), 16)

        def entry(k, acc):
            one = jnp.zeros((16, CY), F32)
            two = jnp.zeros((16, CY), F32)
            for f in range(FREQ):
                re = fwd[f, 0, k, rows].astype(F32)
                im = fwd[f, 1, k, rows].astype(F32)
                acc = acc + (re * adj[f, 0, k, rows] - im * adj[f, 1, k, rows])
                one = one + (cosines[0][f] * re + sines[0][f] * im)
                two = two + (cosines[1][f] * re + sines[1][f] * im)
            gain[k, 0, rows] = one
            gain[k, 1, rows] = two
            return acc

        inter[rows] = lax.fori_loop(0, 3 * PLANES, entry, jnp.zeros((16, CY), F32))
        return 0

    lax.fori_loop(0, CX // 16, chunk, 0)

    lane = iota((EX, 128), 1)
    slot_of = lax.rem(lane, ZL)
    half_sum_scale = math.tanh(sharpness * threshold) + math.tanh(sharpness * (1.0 - threshold))

    def places(columns, width):
        rows = iota((EX, width), 0)
        rows = gx * CX + jnp.where(rows < CX + 4, rows, rows - EX)
        inside = (rows >= 0) & (rows < total_x) & (columns >= 0) & (columns < total_y)
        sigma = sigma_peak * (profile(rows.astype(F32), total_x) + profile(columns.astype(F32), total_y))
        part = jnp.where(inside, 1.0 / (1.0 + 0.5 * sigma), 0.0)
        return (1.0 - 0.5 * sigma) * part, courant * part

    damping, coef_h = places(gy * CY + iota((EX, CY), 1), CY)
    damp[...] = damping
    coef[...] = coef_h
    columns = gy * CY + jnp.where(slot_of < 4, slot_of - EDGE, slot_of + (CY - EDGE - 4))
    damp_s, ch_s = places(columns, 128)
    damp_s = jnp.where(slot_of < 8, damp_s, 0.0)
    ch_s = jnp.where(slot_of < 8, ch_s, 0.0)
    inverse = [1.0 / jnp.full((1, 128), table_ref[k], F32) for k in range(MATS)]

    each_slot(lambda slot: remote(name_out, name_in.at[slot], name_send.at[0], name_recv.at[slot], other).wait_recv())
    K = slots * 8
    P_rows = G * Zn * 2
    per = Zn * 2
    found = jnp.zeros((8, 128), F32)
    for slot in range(slots):
        part = name_in[slot]
        part = pltpu.roll(part, 8 * slot, 1) if slot else part
        found = jnp.where((lane8 >= 8 * slot) & (lane8 < 8 * slot + 8), part, found)
    shift = K
    while shift < 128:
        found = jnp.where(lane8 < shift, found, pltpu.roll(found, shift, 1))
        shift *= 2
    found = jnp.broadcast_to(found[0:1], (P_rows, 128))
    row = iota((P_rows, 128), 0)
    column = iota((P_rows, 128), 1)
    q = row // per
    place = lax.rem(row, per)
    fixed = (1 - core) * (x * 2) + core * (y * (2 * G))
    param = (place // 2) * (2 * G * G) + lax.rem(place, 2) + q * ((1 - core) * (2 * G) + core * 2) + fixed
    match = found == param.astype(F32)
    even_cells = lax.rem(column, 8) < 4
    both = jnp.concatenate(
        [jnp.where(match & even_cells, 1.0, 0.0), jnp.where(match & (~even_cells), 1.0, 0.0)], axis=0
    )
    if K == 64:
        third = jnp.where(iota((2 * P_rows, 128), 1) < 3 * K - 128, both, 0.0)
        chosen = jnp.concatenate([both, third], axis=1).astype(BF16)
    else:
        chosen = jnp.where(iota((2 * P_rows, 128), 1) < 3 * K, both, 0.0).astype(BF16)
    hear_word(0)
    pass_word(1)

    for copy in halos:
        copy.wait_recv()

    def xn(f):
        return pltpu.roll(f, EX - 1, 0)

    def xp(f):
        return pltpu.roll(f, 1, 0)

    def yn(f, strip, p):
        a, b = pltpu.roll(f[:, :128], 127, 1), pltpu.roll(f[:, 128:], 127, 1)
        edge = pltpu.roll(strip, (127 - 6 - p * ZL) % 128, 1)
        end = lane == 127
        return jnp.concatenate([jnp.where(end, b, a), jnp.where(end, edge, b)], axis=1)

    def yp(f, strip, p):
        a, b = pltpu.roll(f[:, :128], 1, 1), pltpu.roll(f[:, 128:], 1, 1)
        edge = pltpu.roll(strip, (127 - p * ZL) % 128, 1)
        start = lane == 0
        return jnp.concatenate([jnp.where(start, edge, a), jnp.where(start, a, b)], axis=1)

    wide = iota((8, CY), 0)
    narrow8 = iota((8, 128), 0)
    from_next, from_prev = (wide < 2) & has_next, (wide >= 6) & has_prev

    def x_halo(kind, p):
        if kind == 7:
            first_row, second_row = xnext[0], xnext[1]
            ahead = jnp.where(wide == 0, pltpu.roll(first_row, 1, 0), pltpu.roll(second_row, 2, 0))
            behind = jnp.where(wide == 6, pltpu.roll(xprev[0], 7, 0), xprev[1])
        else:
            g, at, _ = row_slot(False, kind, p)
            ahead = pltpu.roll(xnext[g], (8 - at) % 8, 0) if at else xnext[g]
            g, at, n = row_slot(True, kind, p)
            shift = (8 - n - at) % 8
            behind = pltpu.roll(xprev[g], shift, 0) if shift else xprev[g]
        return jnp.where(from_next, ahead, jnp.where(from_prev, behind, 0.0))

    halo_rows = pl.ds(CX, 8)
    for c in range(3):
        E[c, NZ] = jnp.zeros((EX, CY), F32)
        H[c, 0] = jnp.zeros((EX, CY), F32)
        for p in range(NZ):
            E[c, p, halo_rows] = x_halo(c, p)
            H[c, p + 1, halo_rows] = x_halo(3 + c, p)

    pieces = []
    for i, body in enumerate((got[0], own[0], own[1], got[1])):
        rim = jnp.where((narrow8 < 4) & has_next, halo_next[i], jnp.where((narrow8 >= 4) & has_prev, halo_prev[i], 0.0))
        piece = jnp.concatenate([body, rim], axis=0)
        if i == 0:
            piece = jnp.where(has_left, piece, 0.0)
        if i == 3:
            piece = jnp.where(has_right, piece, 0.0)
        pieces.append(piece)

    def strip(kind):
        value = jnp.zeros((EX, 128), F32)
        for i, piece in enumerate(pieces):
            shift = (EDGE * i - EDGE * kind) % 128
            moved = pltpu.roll(piece, shift, 1) if shift else piece
            value = jnp.where((slot_of >= EDGE * i) & (slot_of < EDGE * (i + 1)), moved, value)
        return value

    def design(filtered):
        bend = jnp.tanh(sharpness * (filtered - threshold))
        projected = (math.tanh(sharpness * threshold) + bend) / half_sum_scale
        return bend, eps_low + (eps_high - eps_low) * projected

    dens = jnp.concatenate([den[...], x_halo(7, 0)], axis=0)
    dens_s = strip(7)
    dens = xp(dens) + 2.0 * dens + xn(dens)
    dens_s = xp(dens_s) + 2.0 * dens_s + xn(dens_s)
    bend, eps = design((yp(dens, dens_s, ZLO) + 2.0 * dens + yn(dens, dens_s, ZLO)) / 16.0)
    slope[...] = (sharpness * (1.0 - bend * bend) / half_sum_scale)[:CX]
    design_coef = coef[...] / eps
    for p in range(NZ):
        if ZLO <= p < ZLO + PLANES:
            CE[p] = design_coef
        else:
            mats = jnp.concatenate([mat[p].astype(F32), x_halo(6, p)], axis=0)
            part = jnp.broadcast_to(inverse[MATS - 1][:, :1], (EX, CY))
            for k in range(MATS - 1):
                part = jnp.where(mats == float(k), inverse[k][:, :1], part)
            CE[p] = coef[...] * part
    eps_s = design((pltpu.roll(dens_s, 1, 1) + 2.0 * dens_s + pltpu.roll(dens_s, 127, 1)) / 16.0)[1]
    mats = strip(6)
    part = jnp.broadcast_to(inverse[MATS - 1], (EX, 128))
    for k in range(MATS - 1):
        part = jnp.where(mats == float(k), inverse[k], part)
    layer = (lane >= ZLO * ZL) & (lane < (ZLO + PLANES) * ZL)
    ce_s = ch_s * jnp.where(layer, 1.0 / eps_s, part)

    def yns(f):
        return pltpu.roll(f, 127, 1)

    def yps(f):
        return pltpu.roll(f, 1, 1)

    def zns(f):
        return jnp.where(lane < 128 - ZL, pltpu.roll(f, 128 - ZL, 1), 0.0)

    def zps(f):
        return jnp.where(lane >= ZL, pltpu.roll(f, ZL, 1), 0.0)

    def strip_h(ex, ey, ez, hx, hy, hz):
        cx = (yns(ez) - ez) - (zns(ey) - ey)
        cy = (zns(ex) - ex) - (xn(ez) - ez)
        cz = (xn(ey) - ey) - (yns(ex) - ex)
        return damp_s * hx - ch_s * cx, damp_s * hy - ch_s * cy, damp_s * hz - ch_s * cz

    def strip_e(ex, ey, ez, hx, hy, hz):
        cx = (hz - yps(hz)) - (hy - zps(hy))
        cy = (hx - zps(hx)) - (hz - xp(hz))
        cz = (hy - xp(hy)) - (hx - yps(hx))
        return damp_s * ex + ce_s * cx, damp_s * ey + ce_s * cy, damp_s * ez + ce_s * cz

    es = tuple(strip(c) for c in range(3))
    hs = tuple(strip(c) for c in range(3, 6))
    strips[0], strips[1] = es[0], es[2]
    hs = strip_h(*es, *hs)
    strips[2], strips[3] = hs[0], hs[2]
    es = strip_e(*es, *hs)
    strips[4], strips[5] = es[0], es[2]
    hs = strip_h(*es, *hs)
    strips[6], strips[7] = hs[0], hs[2]

    def half_h(p, n):
        ex, ey, ez = E[0, p], E[1, p], E[2, p]
        d, c = damp[...], coef[...]
        hx = d * H[0, p + 1] - c * ((yn(ez, strips[4 * n + 1], p) - ez) - (E[1, p + 1] - ey))
        hy = d * H[1, p + 1] - c * ((E[0, p + 1] - ex) - (xn(ez) - ez))
        hz = d * H[2, p + 1] - c * ((xn(ey) - ey) - (yn(ex, strips[4 * n], p) - ex))
        for i, value in enumerate((hx, hy, hz)):
            H[i, p + 1] = value
            if n:
                h_out[i, p] = value[:CX]

    def half_e(p, n):
        hx, hy, hz = H[0, p + 1], H[1, p + 1], H[2, p + 1]
        d, c = damp[...], CE[p]
        ex = d * E[0, p] + c * ((hz - yp(hz, strips[4 * n + 3], p)) - (hy - H[1, p]))
        ey = d * E[1, p] + c * ((hx - H[0, p]) - (hz - xp(hz)))
        ez = d * E[2, p] + c * ((hy - xp(hy)) - (hx - yp(hx, strips[4 * n + 2], p)))
        acc = inter[...]
        for i, value in enumerate((ex, ey, ez)):
            if n:
                e_out[i, p] = value[:CX]
            else:
                E[i, p] = value
            if ZLO <= p < ZLO + PLANES:
                acc = acc + gain[PLANES * i + (p - ZLO), n] * value[:CX]
        if ZLO <= p < ZLO + PLANES:
            inter[...] = acc

    before, behind_layer = ZLO - 2, ZLO + PLANES
    for p in range(before, behind_layer + 1):
        half_h(p, 0)
        if p > before:
            half_e(p, 0)
        if p > before + 1:
            half_h(p - 1, 1)
        if p > before + 2:
            half_e(p - 1, 1)
    local[...] = grad_scale * (eps_high - eps_low) * slope[...] * inter[...]

    plan = (
        (local.at[bottom, high], corner.at[0], (1, 1)),
        (local.at[bottom, low], corner.at[1], (1, -1)),
        (local.at[top, high], corner.at[2], (-1, 1)),
        (local.at[top, low], corner.at[3], (-1, -1)),
        (local.at[bottom], rim_prev, (1, 0)),
        (local.at[top], rim_next, (-1, 0)),
        (local.at[:, high], rim_left, (0, 1)),
        (local.at[:, low], rim_right, (0, -1)),
    )
    rims = [remote(src, dst, rim_send.at[i], rim_recv.at[i], near[to]) for i, (src, dst, to) in enumerate(plan)]
    for copy in rims:
        copy.start()

    for p in range(behind_layer + 1, NZ + 1):
        if p < NZ:
            half_h(p, 0)
            half_e(p, 0)
        half_h(p - 1, 1)
        half_e(p - 1, 1)

    for copy in rims:
        copy.wait_recv()
    hear_word(1)
    pass_word(2)

    rows = jnp.where((wide < 4) & has_next, rim_next[...], jnp.where((wide >= 4) & has_prev, rim_prev[...], 0.0))
    main = jnp.concatenate([local[...], rows], axis=0)
    left = jnp.concatenate(
        [
            rim_left[...],
            jnp.where((narrow8 < 4) & has_next, corner[2], jnp.where((narrow8 >= 4) & has_prev, corner[0], 0.0)),
        ],
        axis=0,
    )
    left = jnp.where(has_left, left, 0.0)
    right = jnp.concatenate(
        [
            rim_right[...],
            jnp.where((narrow8 < 4) & has_next, corner[3], jnp.where((narrow8 >= 4) & has_prev, corner[1], 0.0)),
        ],
        axis=0,
    )
    right = jnp.where(has_right, right, 0.0)

    def along_x(f):
        return pltpu.roll(f, 1, 0) + 2.0 * f + pltpu.roll(f, EX - 1, 0)

    a, b = along_x(main[:, :128]), along_x(main[:, 128:])
    left, right = along_x(left), along_x(right)
    first, last = lane == 0, lane == 127
    ra, rb = pltpu.roll(a, 1, 1), pltpu.roll(b, 1, 1)
    la, lb = pltpu.roll(a, 127, 1), pltpu.roll(b, 127, 1)
    left, right = pltpu.roll(left, 1, 1), pltpu.roll(right, 127, 1)
    a = (jnp.where(first, left, ra) + 2.0 * a + jnp.where(last, lb, la)) / 16.0
    b = (jnp.where(first, ra, rb) + 2.0 * b + jnp.where(last, right, lb)) / 16.0
    cells[0] = a[:CX]
    cells[1] = b[:CX]

    narrow = iota((CX // 2, 128), 1) < TILE
    for j in range(4):
        even = cells[j // 2, pl.ds(0, CX // 2, stride=2), :]
        odd = cells[j // 2, pl.ds(1, CX // 2, stride=2), :]
        if j % 2:
            tile = jnp.where(narrow, pltpu.roll(even, TILE, 1), odd)
        else:
            tile = jnp.where(narrow, even, pltpu.roll(odd, TILE, 1))
        for h in range(2):
            message[h, pl.ds(j, 16, stride=4), :] = tile[16 * h : 16 * h + 16]

    chunk_rows = [pl.ds(32 * ch, 32) for ch in range(2)]
    first_stop = []
    for ch in range(2):
        for i, (h, slot, to) in enumerate(targets):
            copy = remote(
                message.at[h, chunk_rows[ch]], gathered.at[slot, chunk_rows[ch]], a_send.at[ch, i], a_recv.at[ch, slot], to
            )
            copy.start()
            first_stop.append(copy)
    gathered[core] = message[core]

    for p in range(before):
        half_h(p, 0)
    for p in range(before + 1):
        half_e(p, 0)
    for p in range(before + 1):
        half_h(p, 1)
    for p in range(before + 2):
        half_e(p, 1)

    mine = (1 - core) * y + core * x

    def ring(k):
        there = wrapped(mine, k, G)
        return there, dev((1 - core) * x + core * there, (1 - core) * there + core * y, z, core)

    ahead, to_ahead = ring(1)
    behind, to_behind = ring(-1)
    across, _ = ring(2)
    second_stop = []
    for ch in range(2):
        each_slot(
            lambda slot: remote(
                message.at[0, chunk_rows[ch]], gathered.at[slot, chunk_rows[ch]], a_send.at[ch, 0], a_recv.at[ch, slot], other
            ).wait_recv()
        )
        for m in range(4 * ch, 4 * ch + 4):
            data = jnp.concatenate([gathered[slot, pl.ds(8 * m, 8)] for slot in range(slots)], axis=0)
            hi = data.astype(BF16)
            rest = data - hi.astype(F32)
            mid = rest.astype(BF16)
            lo = (rest - mid.astype(F32)).astype(BF16)
            picked = jnp.dot(chosen, jnp.concatenate([hi, mid, lo, hi], axis=0), preferred_element_type=F32)
            for parity in range(2):
                for place_q in range(G):
                    start = parity * P_rows + place_q * per
                    sums[ch, place_q, 2 * (m - 4 * ch) + parity] = picked[start : start + per]
        far, near_by = (to_ahead, to_behind) if ch == 0 else (to_behind, to_ahead)
        straight = behind if ch == 0 else ahead
        second_stop.append(remote(sums.at[ch, across], passing.at[ch], b_send.at[ch, 0], b_recv.at[ch, 0], far))
        second_stop.append(remote(sums.at[ch, straight], direct.at[ch], b_send.at[ch, 1], b_recv.at[ch, 1], near_by))
        second_stop[-2].start()
        second_stop[-1].start()
    for ch in range(2):
        far = to_ahead if ch == 0 else to_behind
        onward = ahead if ch == 0 else behind
        second_stop[2 * ch].wait_recv()
        passing[ch] = passing[ch] + sums[ch, onward]
        copy = remote(passing.at[ch], combined.at[ch], b_send.at[ch, 2], b_recv.at[ch, 2], far)
        copy.start()
        second_stop.append(copy)
    hear_word(2)

    third_stop = []
    for ch in range(2):
        second_stop[2 * ch + 1].wait_recv()
        second_stop[4 + ch].wait_recv()
        for b in range(8):
            value = sums[ch, mine, b] + direct[ch, b] + combined[ch, b]
            ready[ch, pl.ds(b, per, stride=8), :] = value
        eight = pl.ds(8 * ch, 8)
        order = sorted(range(Zn), key=lambda k: -min(k, Zn - k))
        for k in order:
            there = wrapped(z, k, Zn)
            for c in range(2):
                if k == 0 and c == 0:
                    continue
                target = c if k else 1 - core
                start = pl.multiple_of((there * 2 + target) * 8, 8)
                copy = remote(
                    ready.at[ch, pl.ds(start, 8)],
                    landed.at[2 * k + core, eight],
                    c_send.at[ch, 2 * k + c],
                    c_recv.at[ch, 2 * k + core],
                    dev(x, y, there, target),
                )
                copy.start()
                third_stop.append(copy)
        landed[core, eight] = ready[ch, pl.ds(pl.multiple_of((z * 2 + core) * 8, 8), 8)]

    for ch in range(2):
        eight = pl.ds(8 * ch, 8)

        def landing(slot):
            remote(
                ready.at[ch, pl.ds(0, 8)], landed.at[slot, eight], c_send.at[ch, 0], c_recv.at[ch, slot], other
            ).wait_recv()

        landing(1 - core)
        for k in range(1, Zn):
            for c in range(2):
                landing(2 * k + c)
        for h in range(2):
            value = landed[h, eight]
            for k in range(1, Zn):
                value = value + landed[2 * k + h, eight]
            out[pl.ds(16 * h + 8 * ch, 8)] = value
    for copy in halos + rims + name_copies + first_stop + second_stop + third_stop:
        copy.wait_send()


def solve(G, Zn, e, h, mat, den, fwd, adj, table, tile_map):
    per = Zn * 2
    dma = pltpu.SemaphoreType.DMA
    vmem = lambda *shape: pltpu.VMEM(shape, F32)
    smem = pl.BlockSpec(memory_space=pltpu.SMEM)
    return pl.pallas_call(
        functools.partial(solve_kernel, G, Zn),
        name="solve",
        out_shape=(pltpu.VMEM(e.shape, F32), pltpu.VMEM(h.shape, F32), pltpu.VMEM((32, 128), F32)),
        in_specs=[ANY] * 6 + [smem, smem],
        out_specs=(VMEM, VMEM, VMEM),
        scratch_shapes=[
            vmem(3, NZ + 1, EX, CY),
            vmem(3, NZ + 1, EX, CY),
            vmem(NZ, EX, CY),
            pltpu.VMEM(mat.shape, jnp.int32),
            vmem(CX, CY),
            pltpu.VMEM(fwd.shape, BF16),
            pltpu.VMEM(adj.shape, F32),
            vmem(3 * PLANES, STEPS, CX, CY),
            vmem(CX, CY),
            vmem(CX, CY),
            vmem(EX, CY),
            vmem(EX, CY),
            vmem(2, CX, 128),
            vmem(2, CX, 128),
            vmem(4, 8, 128),
            vmem(4, 8, 128),
            vmem(DOWN_GROUPS, 8, CY),
            vmem(UP_GROUPS, 8, CY),
            vmem(DOWN_GROUPS, 8, CY),
            vmem(UP_GROUPS, 8, CY),
            vmem(8, EX, 128),
            vmem(CX, CY),
            vmem(CX, 128),
            vmem(CX, 128),
            vmem(8, CY),
            vmem(8, CY),
            vmem(4, 8, 128),
            vmem(2, CX, 128),
            vmem(2, CX, 128),
            vmem(8, 128),
            vmem(2 * G, 8, 128),
            vmem(2 * G, CX, 128),
            vmem(2, G, 8, per, 128),
            vmem(2, 8, per, 128),
            vmem(2, 8, per, 128),
            vmem(2, 8, per, 128),
            vmem(2, per * 8, 128),
            vmem(2 * Zn, 16, 128),
            dma((2 * NZ + 4,)),
            dma((10,)),
            dma((10,)),
            dma((8,)),
            dma((8,)),
            dma((2 * G,)),
            dma((2 * G,)),
            dma((2, 2 * G)),
            dma((2, 2 * G)),
            dma((2, 3)),
            dma((2, 3)),
            dma((2, 2 * Zn)),
            dma((2, 2 * Zn)),
            pltpu.SemaphoreType.REGULAR((3,)),
        ],
        compiler_params=pltpu.CompilerParams(collective_id=0, has_side_effects=True),
    )(e, h, mat, den, fwd, adj, table, tile_map)


def on_device(nx, ny, e_adj, h_adj, density, material, eps_table, dft_adj, dft_fwd, tile_map):
    G = ny // 2
    flat = lambda array: array.reshape(FREQ, 2, 3 * PLANES, CX, CY)
    e_out, h_out, params = solve(
        G, nx // G, e_adj, h_adj, material, density, flat(dft_fwd), flat(dft_adj), eps_table, tile_map
    )
    return e_out, h_out, params.reshape(1, TILE * TILE)


def solution(mesh):
    in_specs = (
        P(None, None, "gx", "gy"),
        P(None, None, "gx", "gy"),
        P("gx", "gy"),
        P(None, "gx", "gy"),
        P(),
        P(None, None, None, None, "gx", "gy"),
        P(None, None, None, None, "gx", "gy"),
        P("gx", "gy"),
    )
    out_specs = (P(None, None, "gx", "gy"), P(None, None, "gx", "gy"), P(("gx", "gy"), None))
    return jax.shard_map(
        functools.partial(on_device, mesh.shape["gx"], mesh.shape["gy"]),
        mesh=mesh,
        in_specs=in_specs,
        out_specs=out_specs,
        check_vma=False,
    )
```

time: 435 us -> 44 us (0.10)
  waiting for transfers between devices: 279 us -> 0 us
  starting transfers between devices: 48 us -> 0 us
  local copies, waits for them, and re-layouts: 46.8 us -> 2.89 us
  Pallas kernels: 0 us -> 40.3 us
  other arithmetic: 40 us -> 0 us
  between operations: 14.9 us -> 0.64 us
    unnamed x2 -> x0, waiting for transfers between devices: 269 us -> none
    ppermute x16 -> x0, starting transfers between devices: 48 us -> none  [the longest x8 25.8 us: shifted(): return lax.ppermute(block, axis, route)]
    pallas_call x0 -> x1, Pallas kernels: none -> 40.3 us  [solve(): pl.pallas_call(functools.partial(solve_kernel, G, Zn), name='solve', out_...]
    slice x42 -> x0, local copies, waits for them, and re-layouts: 29.7 us -> none  [the longest x12 12.8 us: step_next(): inner = lax.slice_in_dim(values, 1, values.shape[dim_index], axis=dim_index)]
    another operation x16 -> x0, other arithmetic: 15.2 us -> none  [the longest x4 12.9 us: on_device(): jnp.stack([elec_x, elec_y, elec_z])]
    add x8 -> x0, other arithmetic: 13.6 us -> none  [the longest x1 4.75 us: on_device(): elec_z = damping * elec_z + coef_e * curl_z]
    ppermute x16 -> x0, waiting for transfers between devices: 10.1 us -> none  [the longest x4 8.75 us: with_halo(): lax.ppermute(head, axis, [((i + 1) % count, i) for i in range(ends)])]
    sub x2 -> x0, other arithmetic: 8.14 us -> none  [on_device(): mag_x = damping * mag_x - coef_h * curl_x]
  transfers between devices with their start and end apart: 17 -> 0, of which waited for: 4 -> 0; matrix products, arithmetic and copies ran while one was open for 11% -> 0% of each run, Pallas kernels for 0% -> 0%
where the time goes in v3:
time: 44 us; the launch traced here: 43.9 us
  Pallas kernels  40.3 us (92%)
  local copies, waits for them, and re-layouts  2.89 us (7%)
  between operations  0.64 us (1%)
    pallas_call x1, Pallas kernels, solve(): pl.pallas_call(functools.partial(solve_kernel, G, Zn), name='solve', out_...  40.3 us
    unnamed x3, local copies, waits for them, and re-layouts  2.89 us

profile of v3, /device:TPU:1, one launch (start us, length us, event | category | flops | bytes accessed | tf_op | source)
XLA Modules:
  0.0 43.9 jit_solution(17308067466061608252)
XLA Ops:
  0.6 40.3 %solve.1 = (f32[3,8,64,256]{3,2,1,0:T(8,128)S(1)}, f32[3,8,64,256]{3,2,1,0:T(8,128)S(1)}, f32[32,128]{1,0:T(8,128)S(1)}) custom-call(f32[3,8,64,256]{3,2,1,0:T(8,128)} %e_hbm.1, f32[3,8,64,256]{3,2,1,0:T(8,128)} %h_hbm.1, s32[8,64,256]{2,1,0:T(8,128)} %mat_hbm.1, f32[64,256]{1,0:T(8,128)} %den_hbm.1, bf16[4,2,6,64,256]{4,3,2,1,0:T(8,128)(2,1)} %bitcast.5, ...), custom_call_target="tpu_custom_call" | custom-call | tf_op jit(solution)/shard_map/solve/pallas_call | solution.py:670
  41.0 1.1 %copy.14 = f32[3,8,64,256]{3,2,1,0:T(8,128)} copy(f32[3,8,64,256]{3,2,1,0:T(8,128)S(1)} %get-tuple-element.9) | data formatting | bytes 3145728
  42.1 0.6 %copy.16 = f32[1,4096]{1,0:T(1,128)} copy(f32[1,4096]{1,0:T(1,128)S(1)} %bitcast.3) | data formatting | bytes 32768
  42.7 1.1 %copy.15 = f32[3,8,64,256]{3,2,1,0:T(8,128)} copy(f32[3,8,64,256]{3,2,1,0:T(8,128)S(1)} %get-tuple-element.10) | data formatting | bytes 3145728

commit v4 on v3

--- a/solution.py
+++ b/solution.py
@@ -67,25 +67,30 @@
     return depth * depth * depth
 
 
-DOWN_GROUPS = NZ + (NZ * 6 + 7) // 8
-UP_GROUPS = NZ + (NZ * 3 + 7) // 8
+ORDER = (1, 2, 3, 4, 5, 6, 0, 7)
+EARLY = 6
+DOWN_EARLY, DOWN_GROUPS = 11, 15
+UP_EARLY, UP_GROUPS = 9, 12
 
 
 def row_slot(down, kind, z):
+    at = ORDER.index(z)
+    early = DOWN_EARLY if down else UP_EARLY
+    start, at, count = (0, at, EARLY) if at < EARLY else (early, at - EARLY, NZ - EARLY)
     if kind < 3:
-        return z, 2 * kind, 2
+        return start + at, 2 * kind, 2
     if kind == 6:
-        return z, 6, 1
+        return start + at, 6, 1
     each = 2 if down else 1
-    row = (3 * z + kind - 3) * each
-    return NZ + row // 8, row % 8, each
+    row = (3 * at + kind - 3) * each
+    return start + count + row // 8, row % 8, each
 
 
 def solve_kernel(
     G, Zn,
-    e_hbm, h_hbm, mat_hbm, den_hbm, fwd_hbm, adj_hbm, table_ref, tile_map,
+    e_hbm, h_hbm, mat_hbm, den_hbm, fwd_hbm, adj_hbm, table_hbm, map_hbm,
     e_out, h_out, out,
-    E, H, CE, mat, den, fwd, adj, gain, inter, slope, damp, coef, own, got, halo_prev, halo_next, xdown, xup, xprev, xnext, strips,
+    table_ref, tile_map, E, H, CE, mat, den, fwd, adj, gain, inter, slope, damp, coef, own, got, halo_prev, halo_next, xdown, xup, xprev, xnext, strips,
     local, rim_left, rim_right, rim_prev, rim_next, corner, cells, message, name_out, name_in, gathered, sums, passing, direct,
     combined, ready, landed,
     load_sem, halo_send, halo_recv,
@@ -116,10 +121,6 @@
     for c in range(2):
         partners.append(dev(x, y, above, c))
         partners.append(dev(x, y, below, c))
-    barrier = pltpu.get_barrier_semaphore()
-    for device in partners:
-        signal(barrier, device)
-
     block = pl.ds(0, CX)
     loads = []
 
@@ -130,19 +131,22 @@
         return copy
 
     load_den = load(den_hbm, den)
-    load_mat = load(mat_hbm, mat)
-    load_planes = [
-        (load(e_hbm.at[:, p], E.at[:, p, block]), load(h_hbm.at[:, p], H.at[:, p + 1, block])) for p in range(NZ)
-    ]
-    load_dft = [load(fwd_hbm, fwd), load(adj_hbm, adj)]
-
-    names = jnp.zeros((8, 128), F32)
+    load_small = [load(map_hbm, tile_map), load(table_hbm, table_ref)]
+    load_planes = {
+        p: (
+            load(e_hbm.at[:, p], E.at[:, p, block]),
+            load(h_hbm.at[:, p], H.at[:, p + 1, block]),
+            load(mat_hbm.at[p], mat.at[p]),
+        )
+        for p in ORDER
+    }
+
+    barrier = pltpu.get_barrier_semaphore()
+    for device in partners:
+        signal(barrier, device)
+
+    lane64 = iota((CX, 128), 1)
     lane8 = iota((8, 128), 1)
-    for j in range(4):
-        names = jnp.where(((lane8 == j) | (lane8 == 4 + j)), tile_map[0, j].astype(F32), names)
-    name_out[...] = names
-
-    lane64 = iota((CX, 128), 1)
     low, high, top, bottom = pl.ds(0, 128), pl.ds(128, 128), pl.ds(0, 8), pl.ds(CX - 8, 8)
 
     def plane(kind, p, rows, columns):
@@ -155,15 +159,14 @@
         return den[rows, columns]
 
     load_den.wait()
-    load_mat.wait()
     first = jnp.zeros((CX, 128), F32)
     last = jnp.zeros((CX, 128), F32)
     empty = jnp.zeros((8, CY), F32)
-    for g in range(DOWN_GROUPS - 1, DOWN_GROUPS):
+    for g in range(DOWN_GROUPS):
         xdown[g] = empty
     for g in range(UP_GROUPS):
         xup[g] = empty
-    for p in range(NZ):
+    for p in ORDER:
         for copy in load_planes[p]:
             copy.wait()
         kinds = list(range(7)) + ([7] if ZLO <= p < ZLO + PLANES else [])
@@ -179,11 +182,20 @@
             xdown[g, pl.ds(row, n)] = plane(kind, p, pl.ds(CX - n, n), pl.ds(0, CY))
             g, row, n = row_slot(False, kind, p)
             xup[g, pl.ds(row, n)] = plane(kind, p, pl.ds(0, n), pl.ds(0, CY))
-        xdown[p, pl.ds(7, 1)] = den[pl.ds(CX - 2 + p % 2, 1), :]
-        xup[p, pl.ds(7, 1)] = den[pl.ds(p % 2, 1), :]
+        if p in ORDER[:2]:
+            g = ORDER.index(p)
+            xdown[g, pl.ds(7, 1)] = den[pl.ds(CX - 2 + g, 1), :]
+            xup[g, pl.ds(7, 1)] = den[pl.ds(g, 1), :]
     own[0] = first
     own[1] = last
-
+    load_dft = [load(fwd_hbm, fwd), load(adj_hbm, adj)]
+
+    for copy in load_small:
+        copy.wait()
+    names = jnp.zeros((8, 128), F32)
+    for j in range(4):
+        names = jnp.where(((lane8 == j) | (lane8 == 4 + j)), tile_map[0, j].astype(F32), names)
+    name_out[...] = names
     pl.semaphore_wait(barrier, len(partners))
 
     rounds = Zn // 2 - 1
@@ -198,16 +210,18 @@
             pl.semaphore_wait(heard.at[i], 2)
 
     plan = (
-        (xdown, xprev, (1, 0)),
-        (xup, xnext, (-1, 0)),
-        (own.at[1], got.at[0], (0, 1)),
-        (own.at[0], got.at[1], (0, -1)),
-        (own.at[:, bottom], halo_prev.at[pl.ds(1, 2)], (1, 0)),
-        (own.at[:, top], halo_next.at[pl.ds(1, 2)], (-1, 0)),
         (own.at[1, bottom], halo_prev.at[0], (1, 1)),
         (own.at[0, bottom], halo_prev.at[3], (1, -1)),
         (own.at[1, top], halo_next.at[0], (-1, 1)),
         (own.at[0, top], halo_next.at[3], (-1, -1)),
+        (own.at[:, bottom], halo_prev.at[pl.ds(1, 2)], (1, 0)),
+        (own.at[:, top], halo_next.at[pl.ds(1, 2)], (-1, 0)),
+        (xdown.at[pl.ds(0, DOWN_EARLY)], xprev.at[pl.ds(0, DOWN_EARLY)], (1, 0)),
+        (xup.at[pl.ds(0, UP_EARLY)], xnext.at[pl.ds(0, UP_EARLY)], (-1, 0)),
+        (own.at[1], got.at[0], (0, 1)),
+        (own.at[0], got.at[1], (0, -1)),
+        (xdown.at[pl.ds(DOWN_EARLY, DOWN_GROUPS - DOWN_EARLY)], xprev.at[pl.ds(DOWN_EARLY, DOWN_GROUPS - DOWN_EARLY)], (1, 0)),
+        (xup.at[pl.ds(UP_EARLY, UP_GROUPS - UP_EARLY)], xnext.at[pl.ds(UP_EARLY, UP_GROUPS - UP_EARLY)], (-1, 0)),
     )
     halos = [remote(src, dst, halo_send.at[i], halo_recv.at[i], near[to]) for i, (src, dst, to) in enumerate(plan)]
     for copy in halos:
@@ -315,7 +329,7 @@
     hear_word(0)
     pass_word(1)
 
-    for copy in halos:
+    for copy in halos[:10]:
         copy.wait_recv()
 
     def xn(f):
@@ -342,8 +356,7 @@
 
     def x_halo(kind, p):
         if kind == 7:
-            first_row, second_row = xnext[0], xnext[1]
-            ahead = jnp.where(wide == 0, pltpu.roll(first_row, 1, 0), pltpu.roll(second_row, 2, 0))
+            ahead = jnp.where(wide == 0, pltpu.roll(xnext[0], 1, 0), pltpu.roll(xnext[1], 2, 0))
             behind = jnp.where(wide == 6, pltpu.roll(xprev[0], 7, 0), xprev[1])
         else:
             g, at, _ = row_slot(False, kind, p)
@@ -357,9 +370,14 @@
     for c in range(3):
         E[c, NZ] = jnp.zeros((EX, CY), F32)
         H[c, 0] = jnp.zeros((EX, CY), F32)
-        for p in range(NZ):
-            E[c, p, halo_rows] = x_halo(c, p)
-            H[c, p + 1, halo_rows] = x_halo(3 + c, p)
+
+    def take_halo(planes):
+        for p in planes:
+            for c in range(3):
+                E[c, p, halo_rows] = x_halo(c, p)
+                H[c, p + 1, halo_rows] = x_halo(3 + c, p)
+
+    take_halo(ORDER[:EARLY])
 
     pieces = []
     for i, body in enumerate((got[0], own[0], own[1], got[1])):
@@ -391,15 +409,19 @@
     bend, eps = design((yp(dens, dens_s, ZLO) + 2.0 * dens + yn(dens, dens_s, ZLO)) / 16.0)
     slope[...] = (sharpness * (1.0 - bend * bend) / half_sum_scale)[:CX]
     design_coef = coef[...] / eps
-    for p in range(NZ):
-        if ZLO <= p < ZLO + PLANES:
-            CE[p] = design_coef
-        else:
-            mats = jnp.concatenate([mat[p].astype(F32), x_halo(6, p)], axis=0)
-            part = jnp.broadcast_to(inverse[MATS - 1][:, :1], (EX, CY))
-            for k in range(MATS - 1):
-                part = jnp.where(mats == float(k), inverse[k][:, :1], part)
-            CE[p] = coef[...] * part
+
+    def set_coef(planes):
+        for p in planes:
+            if ZLO <= p < ZLO + PLANES:
+                CE[p] = design_coef
+            else:
+                mats = jnp.concatenate([mat[p].astype(F32), x_halo(6, p)], axis=0)
+                part = jnp.broadcast_to(inverse[MATS - 1][:, :1], (EX, CY))
+                for k in range(MATS - 1):
+                    part = jnp.where(mats == float(k), inverse[k][:, :1], part)
+                CE[p] = coef[...] * part
+
+    set_coef(range(ZLO - 1, ZLO + PLANES + 1))
     eps_s = design((pltpu.roll(dens_s, 1, 1) + 2.0 * dens_s + pltpu.roll(dens_s, 127, 1)) / 16.0)[1]
     mats = strip(6)
     part = jnp.broadcast_to(inverse[MATS - 1], (EX, 128))
@@ -495,6 +517,10 @@
     for copy in rims:
         copy.start()
 
+    for copy in halos[10:]:
+        copy.wait_recv()
+    take_halo(ORDER[EARLY:])
+    set_coef([p for p in range(NZ) if not ZLO - 1 <= p <= ZLO + PLANES])
     for p in range(behind_layer + 1, NZ + 1):
         if p < NZ:
             half_h(p, 0)
@@ -502,68 +528,84 @@
         half_h(p - 1, 1)
         half_e(p - 1, 1)
 
-    for copy in rims:
-        copy.wait_recv()
     hear_word(1)
     pass_word(2)
 
-    rows = jnp.where((wide < 4) & has_next, rim_next[...], jnp.where((wide >= 4) & has_prev, rim_prev[...], 0.0))
-    main = jnp.concatenate([local[...], rows], axis=0)
-    left = jnp.concatenate(
-        [
-            rim_left[...],
-            jnp.where((narrow8 < 4) & has_next, corner[2], jnp.where((narrow8 >= 4) & has_prev, corner[0], 0.0)),
-        ],
-        axis=0,
-    )
-    left = jnp.where(has_left, left, 0.0)
-    right = jnp.concatenate(
-        [
-            rim_right[...],
-            jnp.where((narrow8 < 4) & has_next, corner[3], jnp.where((narrow8 >= 4) & has_prev, corner[1], 0.0)),
-        ],
-        axis=0,
-    )
-    right = jnp.where(has_right, right, 0.0)
-
-    def along_x(f):
-        return pltpu.roll(f, 1, 0) + 2.0 * f + pltpu.roll(f, EX - 1, 0)
-
-    a, b = along_x(main[:, :128]), along_x(main[:, 128:])
-    left, right = along_x(left), along_x(right)
-    first, last = lane == 0, lane == 127
-    ra, rb = pltpu.roll(a, 1, 1), pltpu.roll(b, 1, 1)
-    la, lb = pltpu.roll(a, 127, 1), pltpu.roll(b, 127, 1)
-    left, right = pltpu.roll(left, 1, 1), pltpu.roll(right, 127, 1)
-    a = (jnp.where(first, left, ra) + 2.0 * a + jnp.where(last, lb, la)) / 16.0
-    b = (jnp.where(first, ra, rb) + 2.0 * b + jnp.where(last, right, lb)) / 16.0
-    cells[0] = a[:CX]
-    cells[1] = b[:CX]
-
-    narrow = iota((CX // 2, 128), 1) < TILE
-    for j in range(4):
-        even = cells[j // 2, pl.ds(0, CX // 2, stride=2), :]
-        odd = cells[j // 2, pl.ds(1, CX // 2, stride=2), :]
-        if j % 2:
-            tile = jnp.where(narrow, pltpu.roll(even, TILE, 1), odd)
-        else:
-            tile = jnp.where(narrow, even, pltpu.roll(odd, TILE, 1))
-        for h in range(2):
-            message[h, pl.ds(j, 16, stride=4), :] = tile[16 * h : 16 * h + 16]
-
-    chunk_rows = [pl.ds(32 * ch, 32) for ch in range(2)]
+    def smooth_rows(main, left, right):
+        count = main.shape[0]
+        lanes = iota((count, 128), 1)
+
+        def along_x(f):
+            return pltpu.roll(f, 1, 0) + 2.0 * f + pltpu.roll(f, count - 1, 0)
+
+        a, b = along_x(main[:, :128]), along_x(main[:, 128:])
+        left = pltpu.roll(along_x(jnp.where(has_left, left, 0.0)), 1, 1)
+        right = pltpu.roll(along_x(jnp.where(has_right, right, 0.0)), 127, 1)
+        start, end = lanes == 0, lanes == 127
+        ra, rb = pltpu.roll(a, 1, 1), pltpu.roll(b, 1, 1)
+        la, lb = pltpu.roll(a, 127, 1), pltpu.roll(b, 127, 1)
+        a = (jnp.where(start, left, ra) + 2.0 * a + jnp.where(end, lb, la)) / 16.0
+        b = (jnp.where(start, ra, rb) + 2.0 * b + jnp.where(end, right, lb)) / 16.0
+        return a, b
+
+    def put(at, h, row):
+        slim = iota((8, 128), 1) < TILE
+        for j in range(4):
+            even = cells[j // 2, pl.ds(at, 8, stride=2), :]
+            odd = cells[j // 2, pl.ds(at + 1, 8, stride=2), :]
+            if j % 2:
+                tile = jnp.where(slim, pltpu.roll(even, TILE, 1), odd)
+            else:
+                tile = jnp.where(slim, even, pltpu.roll(odd, TILE, 1))
+            message[h, pl.ds(4 * row + j, 8, stride=4), :] = tile
+
     first_stop = []
-    for ch in range(2):
+
+    def rows_of(turn, h):
+        if isinstance(h, int):
+            return pl.ds(32 * ((turn + 1 - h) % 2), 32)
+        return pl.ds(pl.multiple_of(32 * lax.rem(turn + 1 - h, 2), 32), 32)
+
+    def send_turn(turn):
         for i, (h, slot, to) in enumerate(targets):
+            where = rows_of(turn, h if isinstance(h, int) else 1 - core)
             copy = remote(
-                message.at[h, chunk_rows[ch]], gathered.at[slot, chunk_rows[ch]], a_send.at[ch, i], a_recv.at[ch, slot], to
+                message.at[h, where], gathered.at[slot, where], a_send.at[turn, i], a_recv.at[turn, slot], to
             )
             copy.start()
             first_stop.append(copy)
-    gathered[core] = message[core]
-
+
+    for copy in rims[6:]:
+        copy.wait_recv()
+    inner = pl.ds(8, 48)
+    a, b = smooth_rows(local[inner], rim_left[inner], rim_right[inner])
+    cells[0, inner] = a
+    cells[1, inner] = b
+    put(16, 0, 8)
+    put(32, 1, 0)
+    send_turn(0)
     for p in range(before):
         half_h(p, 0)
+    for copy in rims[:6]:
+        copy.wait_recv()
+    tail, head = pl.ds(40, 24), pl.ds(0, 24)
+    rows = jnp.where((wide < 4) & has_next, rim_next[...], jnp.where((wide >= 4) & has_prev, rim_prev[...], 0.0))
+    side = lambda ahead, back: jnp.where(
+        (narrow8 < 4) & has_next, corner[ahead], jnp.where((narrow8 >= 4) & has_prev, corner[back], 0.0)
+    )
+    a, b = smooth_rows(
+        jnp.concatenate([local[tail], rows, local[head]], axis=0),
+        jnp.concatenate([rim_left[tail], side(2, 0), rim_left[head]], axis=0),
+        jnp.concatenate([rim_right[tail], side(3, 1), rim_right[head]], axis=0),
+    )
+    for i, value in enumerate((a, b)):
+        cells[i, pl.ds(48, 16)] = value[8:24]
+        cells[i, pl.ds(0, 16)] = value[32:48]
+    put(0, 0, 0)
+    put(48, 1, 8)
+    send_turn(1)
+    gathered[core] = message[core]
+
     for p in range(before + 1):
         half_e(p, 0)
     for p in range(before + 1):
@@ -580,49 +622,59 @@
     ahead, to_ahead = ring(1)
     behind, to_behind = ring(-1)
     across, _ = ring(2)
-    second_stop = []
-    for ch in range(2):
+    second_stop = {}
+    for turn in range(2):
+        where = rows_of(turn, core)
         each_slot(
             lambda slot: remote(
-                message.at[0, chunk_rows[ch]], gathered.at[slot, chunk_rows[ch]], a_send.at[ch, 0], a_recv.at[ch, slot], other
+                message.at[0, where], gathered.at[slot, where], a_send.at[turn, 0], a_recv.at[turn, slot], other
             ).wait_recv()
         )
-        for m in range(4 * ch, 4 * ch + 4):
-            data = jnp.concatenate([gathered[slot, pl.ds(8 * m, 8)] for slot in range(slots)], axis=0)
-            hi = data.astype(BF16)
-            rest = data - hi.astype(F32)
-            mid = rest.astype(BF16)
-            lo = (rest - mid.astype(F32)).astype(BF16)
-            picked = jnp.dot(chosen, jnp.concatenate([hi, mid, lo, hi], axis=0), preferred_element_type=F32)
-            for parity in range(2):
-                for place_q in range(G):
-                    start = parity * P_rows + place_q * per
-                    sums[ch, place_q, 2 * (m - 4 * ch) + parity] = picked[start : start + per]
-        far, near_by = (to_ahead, to_behind) if ch == 0 else (to_behind, to_ahead)
-        straight = behind if ch == 0 else ahead
-        second_stop.append(remote(sums.at[ch, across], passing.at[ch], b_send.at[ch, 0], b_recv.at[ch, 0], far))
-        second_stop.append(remote(sums.at[ch, straight], direct.at[ch], b_send.at[ch, 1], b_recv.at[ch, 1], near_by))
-        second_stop[-2].start()
-        second_stop[-1].start()
-    for ch in range(2):
-        far = to_ahead if ch == 0 else to_behind
-        onward = ahead if ch == 0 else behind
-        second_stop[2 * ch].wait_recv()
-        passing[ch] = passing[ch] + sums[ch, onward]
-        copy = remote(passing.at[ch], combined.at[ch], b_send.at[ch, 2], b_recv.at[ch, 2], far)
-        copy.start()
-        second_stop.append(copy)
+        offset = 32 * lax.rem(turn + 1 - core, 2)
+        for way in range(2):
+            for m in range(2 * way, 2 * way + 2):
+                eight = pl.ds(pl.multiple_of(offset + 8 * m, 8), 8)
+                data = jnp.concatenate([gathered[slot, eight] for slot in range(slots)], axis=0)
+                hi = data.astype(BF16)
+                rest = data - hi.astype(F32)
+                mid = rest.astype(BF16)
+                lo = (rest - mid.astype(F32)).astype(BF16)
+                picked = jnp.dot(chosen, jnp.concatenate([hi, mid, lo, hi], axis=0), preferred_element_type=F32)
+                for parity in range(2):
+                    for place_q in range(G):
+                        start = parity * P_rows + place_q * per
+                        sums[turn, way, place_q, 2 * (m - 2 * way) + parity] = picked[start : start + per]
+            far, near_by = (to_ahead, to_behind) if way == 0 else (to_behind, to_ahead)
+            straight = behind if way == 0 else ahead
+            for kind, src, dst, to in ((0, across, passing, far), (1, straight, direct, near_by)):
+                copy = remote(
+                    sums.at[turn, way, src], dst.at[turn, way], b_send.at[turn, way, kind], b_recv.at[turn, way, kind], to
+                )
+                copy.start()
+                second_stop[turn, way, kind] = copy
+    for turn in range(2):
+        for way in range(2):
+            far = to_ahead if way == 0 else to_behind
+            onward = ahead if way == 0 else behind
+            second_stop[turn, way, 0].wait_recv()
+            passing[turn, way] = passing[turn, way] + sums[turn, way, onward]
+            copy = remote(
+                passing.at[turn, way], combined.at[turn, way], b_send.at[turn, way, 2], b_recv.at[turn, way, 2], far
+            )
+            copy.start()
+            second_stop[turn, way, 2] = copy
     hear_word(2)
 
     third_stop = []
-    for ch in range(2):
-        second_stop[2 * ch + 1].wait_recv()
-        second_stop[4 + ch].wait_recv()
-        for b in range(8):
-            value = sums[ch, mine, b] + direct[ch, b] + combined[ch, b]
-            ready[ch, pl.ds(b, per, stride=8), :] = value
-        eight = pl.ds(8 * ch, 8)
-        order = sorted(range(Zn), key=lambda k: -min(k, Zn - k))
+    order = sorted(range(Zn), key=lambda k: -min(k, Zn - k))
+    for turn in range(2):
+        for way in range(2):
+            second_stop[turn, way, 1].wait_recv()
+            second_stop[turn, way, 2].wait_recv()
+            for b in range(4):
+                value = sums[turn, way, mine, b] + direct[turn, way, b] + combined[turn, way, b]
+                ready[turn, pl.ds(4 * way + b, per, stride=8), :] = value
+        eight = pl.ds(8 * turn, 8)
         for k in order:
             there = wrapped(z, k, Zn)
             for c in range(2):
@@ -631,22 +683,22 @@
                 target = c if k else 1 - core
                 start = pl.multiple_of((there * 2 + target) * 8, 8)
                 copy = remote(
-                    ready.at[ch, pl.ds(start, 8)],
+                    ready.at[turn, pl.ds(start, 8)],
                     landed.at[2 * k + core, eight],
-                    c_send.at[ch, 2 * k + c],
-                    c_recv.at[ch, 2 * k + core],
+                    c_send.at[turn, 2 * k + c],
+                    c_recv.at[turn, 2 * k + core],
                     dev(x, y, there, target),
                 )
                 copy.start()
                 third_stop.append(copy)
-        landed[core, eight] = ready[ch, pl.ds(pl.multiple_of((z * 2 + core) * 8, 8), 8)]
-
-    for ch in range(2):
-        eight = pl.ds(8 * ch, 8)
+        landed[core, eight] = ready[turn, pl.ds(pl.multiple_of((z * 2 + core) * 8, 8), 8)]
+
+    for turn in range(2):
+        eight = pl.ds(8 * turn, 8)
 
         def landing(slot):
             remote(
-                ready.at[ch, pl.ds(0, 8)], landed.at[slot, eight], c_send.at[ch, 0], c_recv.at[ch, slot], other
+                ready.at[turn, pl.ds(0, 8)], landed.at[slot, eight], c_send.at[turn, 0], c_recv.at[turn, slot], other
             ).wait_recv()
 
         landing(1 - core)
@@ -657,8 +709,8 @@
             value = landed[h, eight]
             for k in range(1, Zn):
                 value = value + landed[2 * k + h, eight]
-            out[pl.ds(16 * h + 8 * ch, 8)] = value
-    for copy in halos + rims + name_copies + first_stop + second_stop + third_stop:
+            out[pl.ds(16 * h + 8 * ((turn + 1 - h) % 2), 8)] = value
+    for copy in halos + rims + name_copies + first_stop + list(second_stop.values()) + third_stop:
         copy.wait_send()
 
 
@@ -666,14 +718,15 @@
     per = Zn * 2
     dma = pltpu.SemaphoreType.DMA
     vmem = lambda *shape: pltpu.VMEM(shape, F32)
-    smem = pl.BlockSpec(memory_space=pltpu.SMEM)
     return pl.pallas_call(
         functools.partial(solve_kernel, G, Zn),
         name="solve",
         out_shape=(pltpu.VMEM(e.shape, F32), pltpu.VMEM(h.shape, F32), pltpu.VMEM((32, 128), F32)),
-        in_specs=[ANY] * 6 + [smem, smem],
+        in_specs=[ANY] * 8,
         out_specs=(VMEM, VMEM, VMEM),
         scratch_shapes=[
+            pltpu.SMEM(table.shape, F32),
+            pltpu.SMEM(tile_map.shape, jnp.int32),
             vmem(3, NZ + 1, EX, CY),
             vmem(3, NZ + 1, EX, CY),
             vmem(NZ, EX, CY),
@@ -706,23 +759,23 @@
             vmem(8, 128),
             vmem(2 * G, 8, 128),
             vmem(2 * G, CX, 128),
-            vmem(2, G, 8, per, 128),
-            vmem(2, 8, per, 128),
-            vmem(2, 8, per, 128),
-            vmem(2, 8, per, 128),
+            vmem(2, 2, G, 4, per, 128),
+            vmem(2, 2, 4, per, 128),
+            vmem(2, 2, 4, per, 128),
+            vmem(2, 2, 4, per, 128),
             vmem(2, per * 8, 128),
             vmem(2 * Zn, 16, 128),
-            dma((2 * NZ + 4,)),
-            dma((10,)),
-            dma((10,)),
+            dma((3 * NZ + 5,)),
+            dma((12,)),
+            dma((12,)),
             dma((8,)),
             dma((8,)),
             dma((2 * G,)),
             dma((2 * G,)),
             dma((2, 2 * G)),
             dma((2, 2 * G)),
-            dma((2, 3)),
-            dma((2, 3)),
+            dma((2, 2, 3)),
+            dma((2, 2, 3)),
             dma((2, 2 * Zn)),
             dma((2, 2 * Zn)),
             pltpu.SemaphoreType.REGULAR((3,)),
@@ -731,12 +784,39 @@
     )(e, h, mat, den, fwd, adj, table, tile_map)
 
 
+def write_kernel(e, h, params, e_out, h_out, params_out, sems):
+    copies = []
+    for src, dst in ((e, e_out), (h, h_out)):
+        for c in range(3):
+            for half in range(2):
+                part = pl.ds(half * (NZ // 2), NZ // 2)
+                copies.append(pltpu.make_async_copy(src.at[c, part], dst.at[c, part], sems.at[len(copies)]))
+    copies.append(pltpu.make_async_copy(params, params_out, sems.at[len(copies)]))
+    for copy in copies:
+        copy.start()
+    for copy in copies:
+        copy.wait()
+
+
+def write(e, h, params):
+    shape = jax.ShapeDtypeStruct
+    return pl.pallas_call(
+        write_kernel,
+        name="write",
+        out_shape=tuple(shape(array.shape, F32) for array in (e, h, params)),
+        in_specs=[VMEM] * 3,
+        out_specs=(ANY,) * 3,
+        scratch_shapes=[pltpu.SemaphoreType.DMA((13,))],
+    )(*(pltpu.with_memory_space_constraint(array, pltpu.VMEM) for array in (e, h, params)))
+
+
 def on_device(nx, ny, e_adj, h_adj, density, material, eps_table, dft_adj, dft_fwd, tile_map):
     G = ny // 2
     flat = lambda array: array.reshape(FREQ, 2, 3 * PLANES, CX, CY)
     e_out, h_out, params = solve(
         G, nx // G, e_adj, h_adj, material, density, flat(dft_fwd), flat(dft_adj), eps_table, tile_map
     )
+    e_out, h_out, params = write(e_out, h_out, params)
     return e_out, h_out, params.reshape(1, TILE * TILE)
 
 

time: 44 us -> 41.3 us (0.939)
  local copies, waits for them, and re-layouts: 2.89 us -> 0 us
    unnamed x3 -> x0, local copies, waits for them, and re-layouts: 2.89 us -> none
    pallas_call x0 -> x1, Pallas kernels: none -> 1.77 us  [write(): pl.pallas_call(write_kernel, name='write', out_shape=tuple((shape(array.s...]
    pallas_call x1, Pallas kernels: 40.3 us -> 38.8 us  [solve(): pl.pallas_call(functools.partial(solve_kernel, G, Zn), name='solve', out_...]
where the time goes in v4:
time: 41.3 us; the launch traced here: 41.2 us
  Pallas kernels  40.5 us (98%)
  between operations  0.64 us (2%)
    pallas_call x1, Pallas kernels, solve(): pl.pallas_call(functools.partial(solve_kernel, G, Zn), name='solve', out_...  38.8 us
    pallas_call x1, Pallas kernels, write(): pl.pallas_call(write_kernel, name='write', out_shape=tuple((shape(array.s...  1.77 us

profile of v4, /device:TPU:1, one launch (start us, length us, event | category | flops | bytes accessed | tf_op | source)
XLA Modules:
  0.0 41.2 jit_solution(18098438068474599116)
XLA Ops:
  0.6 38.8 %solve.1 = (f32[3,8,64,256]{3,2,1,0:T(8,128)S(1)}, f32[3,8,64,256]{3,2,1,0:T(8,128)S(1)}, f32[32,128]{1,0:T(8,128)S(1)}) custom-call(f32[3,8,64,256]{3,2,1,0:T(8,128)} %e_hbm.1, f32[3,8,64,256]{3,2,1,0:T(8,128)} %h_hbm.1, s32[8,64,256]{2,1,0:T(8,128)} %mat_hbm.1, f32[64,256]{1,0:T(8,128)} %den_hbm.1, bf16[4,2,6,64,256]{4,3,2,1,0:T(8,128)(2,1)} %bitcast.4, ...), custom_call_target="tpu_custom_call" | custom-call | tf_op jit(solution)/shard_map/solve/pallas_call | solution.py:721
  39.4 1.8 %write.1 = (f32[3,8,64,256]{3,2,1,0:T(8,128)}, f32[3,8,64,256]{3,2,1,0:T(8,128)}, f32[32,128]{1,0:T(8,128)}) custom-call(f32[3,8,64,256]{3,2,1,0:T(8,128)S(1)} %get-tuple-element.9.e, f32[3,8,64,256]{3,2,1,0:T(8,128)S(1)} %get-tuple-element.10.h, f32[32,128]{1,0:T(8,128)S(1)} %get-tuple-element.11.params), custom_call_target="tpu_custom_call" | custom-call | tf_op jit(solution)/shard_map/write/pallas_call | solution.py:803

commit v5 on v4

--- a/solution.py
+++ b/solution.py
@@ -673,43 +673,35 @@
             second_stop[turn, way, 2].wait_recv()
             for b in range(4):
                 value = sums[turn, way, mine, b] + direct[turn, way, b] + combined[turn, way, b]
-                ready[turn, pl.ds(4 * way + b, per, stride=8), :] = value
-        eight = pl.ds(8 * turn, 8)
-        for k in order:
-            there = wrapped(z, k, Zn)
-            for c in range(2):
-                if k == 0 and c == 0:
-                    continue
-                target = c if k else 1 - core
-                start = pl.multiple_of((there * 2 + target) * 8, 8)
-                copy = remote(
-                    ready.at[turn, pl.ds(start, 8)],
-                    landed.at[2 * k + core, eight],
-                    c_send.at[turn, 2 * k + c],
-                    c_recv.at[turn, 2 * k + core],
-                    dev(x, y, there, target),
-                )
-                copy.start()
-                third_stop.append(copy)
-        landed[core, eight] = ready[turn, pl.ds(pl.multiple_of((z * 2 + core) * 8, 8), 8)]
-
-    for turn in range(2):
-        eight = pl.ds(8 * turn, 8)
-
-        def landing(slot):
-            remote(
-                ready.at[turn, pl.ds(0, 8)], landed.at[slot, eight], c_send.at[turn, 0], c_recv.at[turn, slot], other
-            ).wait_recv()
-
-        landing(1 - core)
+                ready[pl.ds(8 * turn + 4 * way + b, per, stride=16), :] = value
+    for k in order:
+        there = wrapped(z, k, Zn)
+        for c in range(2):
+            if k == 0 and c == 0:
+                continue
+            target = c if k else 1 - core
+            start = pl.multiple_of((there * 2 + target) * 16, 16)
+            copy = remote(
+                ready.at[pl.ds(start, 16)], landed.at[2 * k + core], c_send.at[2 * k + c], c_recv.at[2 * k + core],
+                dev(x, y, there, target),
+            )
+            copy.start()
+            third_stop.append(copy)
+    landed[core] = ready[pl.ds(pl.multiple_of((z * 2 + core) * 16, 16), 16)]
+
+    def landing(slot):
+        remote(ready.at[pl.ds(0, 16)], landed.at[slot], c_send.at[0], c_recv.at[slot], other).wait_recv()
+
+    landing(1 - core)
+    for k in sorted(range(1, Zn), key=lambda k: min(k, Zn - k)):
+        for c in range(2):
+            landing(2 * k + c)
+    for h in range(2):
+        value = landed[h]
         for k in range(1, Zn):
-            for c in range(2):
-                landing(2 * k + c)
-        for h in range(2):
-            value = landed[h, eight]
-            for k in range(1, Zn):
-                value = value + landed[2 * k + h, eight]
-            out[pl.ds(16 * h + 8 * ((turn + 1 - h) % 2), 8)] = value
+            value = value + landed[2 * k + h]
+        for turn in range(2):
+            out[pl.ds(16 * h + 8 * ((turn + 1 - h) % 2), 8)] = value[8 * turn : 8 * turn + 8]
     for copy in halos + rims + name_copies + first_stop + list(second_stop.values()) + third_stop:
         copy.wait_send()
 
@@ -763,7 +755,7 @@
             vmem(2, 2, 4, per, 128),
             vmem(2, 2, 4, per, 128),
             vmem(2, 2, 4, per, 128),
-            vmem(2, per * 8, 128),
+            vmem(per * 16, 128),
             vmem(2 * Zn, 16, 128),
             dma((3 * NZ + 5,)),
             dma((12,)),
@@ -776,8 +768,8 @@
             dma((2, 2 * G)),
             dma((2, 2, 3)),
             dma((2, 2, 3)),
-            dma((2, 2 * Zn)),
-            dma((2, 2 * Zn)),
+            dma((2 * Zn,)),
+            dma((2 * Zn,)),
             pltpu.SemaphoreType.REGULAR((3,)),
         ],
         compiler_params=pltpu.CompilerParams(collective_id=0, has_side_effects=True),

time: 41.3 us -> 40.8 us (0.988)
    pallas_call x1, Pallas kernels: 38.8 us -> 38.3 us  [solve(): pl.pallas_call(functools.partial(solve_kernel, G, Zn), name='solve', out_...]
where the time goes in v5:
time: 40.8 us
  Pallas kernels  40.1 us (98%)
  between operations  0.64 us (2%)
    pallas_call x1, Pallas kernels, solve(): pl.pallas_call(functools.partial(solve_kernel, G, Zn), name='solve', out_...  38.3 us
    pallas_call x1, Pallas kernels, write(): pl.pallas_call(write_kernel, name='write', out_shape=tuple((shape(array.s...  1.77 us

profile of v5, /device:TPU:1, one launch (start us, length us, event | category | flops | bytes accessed | tf_op | source)
XLA Modules:
  0.0 40.8 jit_solution(9430500342133947308)
XLA Ops:
  0.6 38.3 %solve.1 = (f32[3,8,64,256]{3,2,1,0:T(8,128)S(1)}, f32[3,8,64,256]{3,2,1,0:T(8,128)S(1)}, f32[32,128]{1,0:T(8,128)S(1)}) custom-call(f32[3,8,64,256]{3,2,1,0:T(8,128)} %e_hbm.1, f32[3,8,64,256]{3,2,1,0:T(8,128)} %h_hbm.1, s32[8,64,256]{2,1,0:T(8,128)} %mat_hbm.1, f32[64,256]{1,0:T(8,128)} %den_hbm.1, bf16[4,2,6,64,256]{4,3,2,1,0:T(8,128)(2,1)} %bitcast.4, ...), custom_call_target="tpu_custom_call" | custom-call | tf_op jit(solution)/shard_map/solve/pallas_call | solution.py:713
  39.0 1.8 %write.1 = (f32[3,8,64,256]{3,2,1,0:T(8,128)}, f32[3,8,64,256]{3,2,1,0:T(8,128)}, f32[32,128]{1,0:T(8,128)}) custom-call(f32[3,8,64,256]{3,2,1,0:T(8,128)S(1)} %get-tuple-element.9.e, f32[3,8,64,256]{3,2,1,0:T(8,128)S(1)} %get-tuple-element.10.h, f32[32,128]{1,0:T(8,128)S(1)} %get-tuple-element.11.params), custom_call_target="tpu_custom_call" | custom-call | tf_op jit(solution)/shard_map/write/pallas_call | solution.py:795

commit v6 on v5

--- a/solution.py
+++ b/solution.py
@@ -188,7 +188,6 @@
             xup[g, pl.ds(7, 1)] = den[pl.ds(g, 1), :]
     own[0] = first
     own[1] = last
-    load_dft = [load(fwd_hbm, fwd), load(adj_hbm, adj)]
 
     for copy in load_small:
         copy.wait()
@@ -248,6 +247,8 @@
         for k in range(1, G):
             for c in range(2):
                 wait(2 * k + c)
+
+    load_dft = [load(fwd_hbm, fwd), load(adj_hbm, adj)]
 
     for copy in load_dft:
         copy.wait()
@@ -692,6 +693,8 @@
     def landing(slot):
         remote(ready.at[pl.ds(0, 16)], landed.at[slot], c_send.at[0], c_recv.at[slot], other).wait_recv()
 
+    for copy in halos + rims + name_copies + first_stop + list(second_stop.values()):
+        copy.wait_send()
     landing(1 - core)
     for k in sorted(range(1, Zn), key=lambda k: min(k, Zn - k)):
         for c in range(2):
@@ -702,7 +705,7 @@
             value = value + landed[2 * k + h]
         for turn in range(2):
             out[pl.ds(16 * h + 8 * ((turn + 1 - h) % 2), 8)] = value[8 * turn : 8 * turn + 8]
-    for copy in halos + rims + name_copies + first_stop + list(second_stop.values()) + third_stop:
+    for copy in third_stop:
         copy.wait_send()
 
 

time: 40.8 us -> 40.8 us (level)
  no operation moved by 1% of the time
where the time goes in v6:
time: 40.8 us; the launch traced here: 40.7 us
  Pallas kernels  40 us (98%)
  between operations  0.64 us (2%)
    pallas_call x1, Pallas kernels, solve(): pl.pallas_call(functools.partial(solve_kernel, G, Zn), name='solve', out_...  38.3 us
    pallas_call x1, Pallas kernels, write(): pl.pallas_call(write_kernel, name='write', out_shape=tuple((shape(array.s...  1.77 us

profile of v6, /device:TPU:1, one launch (start us, length us, event | category | flops | bytes accessed | tf_op | source)
XLA Modules:
  0.0 40.7 jit_solution(5653409886665301734)
XLA Ops:
  0.6 38.3 %solve.1 = (f32[3,8,64,256]{3,2,1,0:T(8,128)S(1)}, f32[3,8,64,256]{3,2,1,0:T(8,128)S(1)}, f32[32,128]{1,0:T(8,128)S(1)}) custom-call(f32[3,8,64,256]{3,2,1,0:T(8,128)} %e_hbm.1, f32[3,8,64,256]{3,2,1,0:T(8,128)} %h_hbm.1, s32[8,64,256]{2,1,0:T(8,128)} %mat_hbm.1, f32[64,256]{1,0:T(8,128)} %den_hbm.1, bf16[4,2,6,64,256]{4,3,2,1,0:T(8,128)(2,1)} %bitcast.4, ...), custom_call_target="tpu_custom_call" | custom-call | tf_op jit(solution)/shard_map/solve/pallas_call | solution.py:716
  38.9 1.8 %write.1 = (f32[3,8,64,256]{3,2,1,0:T(8,128)}, f32[3,8,64,256]{3,2,1,0:T(8,128)}, f32[32,128]{1,0:T(8,128)}) custom-call(f32[3,8,64,256]{3,2,1,0:T(8,128)S(1)} %get-tuple-element.9.e, f32[3,8,64,256]{3,2,1,0:T(8,128)S(1)} %get-tuple-element.10.h, f32[32,128]{1,0:T(8,128)S(1)} %get-tuple-element.11.params), custom_call_target="tpu_custom_call" | custom-call | tf_op jit(solution)/shard_map/write/pallas_call | solution.py:798
